TPU v7x, 256 devices: a whole 4x4x8 slice. The times are simulated.
256 devices in a mesh: section: 4 (over x), shard: 64 (over z, y, core).
Axes of the slice: x: 4, y: 4, z: 8, core: 2. Of those that a mesh axis runs over, the one named last changes fastest.
Arguments:
- voltages: bfloat16 [4, 2, 1024, 32768], P('section', None, 'shard'), may hold values from -30 to 30, as said below
- feed_gains: bfloat16 [2, 1024, 1024], P(None, 'shard'), may hold values from -6 to 6
- grid_index: int32 [1024], replicated, may hold values from 0 to 1023, each once
- decay_rates: float32 [1024], P('shard'), may hold values from 0.3 to 0.95
- delays: int32 [1024, 512], replicated, may hold values from 0 to 4095
Outputs:
- dedispersed: bfloat16 [4, 7, 512, 2, 1024], P('section', None, None, None, 'shard')
Inputs may be any that keep to these rules, and one draw needn't show every extreme that they name: Real sample voltages.
All inputs are finite; a program needn't handle non-finite values.
Results may differ from a plain program's by a relative error of at most 0.009.
Values may be sent and summed in bfloat16 or wider, within the bound.
A program may use at most 192 MiB of HBM per device.

v0:
```python
import math

import jax
import jax.numpy as jnp
import numpy as np
from jax import lax
from jax.sharding import PartitionSpec as P

POL = 2
GRID_X = 4
GRID_Y = 256
NSAMP = 2048
TDFT = 16
FEEDS = 1024
CHANS = 1024
MODF = 7


def carried_in(part, axis, combine, identity):
    place = lax.axis_index(axis)
    gathered = jax.tree.map(lambda a: lax.all_gather(a, axis), part)
    state = jax.tree.map(lambda a, e: jnp.zeros_like(a) + jnp.asarray(e, a.dtype), part, identity)

    def one(lap, state):
        return combine(
            state, jax.tree.map(lambda a: lax.dynamic_index_in_dim(a, lap, 0, False), gathered)
        )

    return lax.fori_loop(0, place, one, state)


def spectral_constant():
    row_index = np.arange(CHANS, dtype=np.int64)[:, None]
    col_index = np.arange(NSAMP, dtype=np.int64)[None, :]
    angles = np.float32(2.0 * math.pi / NSAMP) * (row_index * col_index % NSAMP).astype(np.float32)
    table = np.concatenate([np.cos(angles), -np.sin(angles)], 0).astype(np.float32)
    return jnp.asarray(table).astype(jnp.bfloat16)


def twiddle_table(length):
    row_index = jnp.arange(length, dtype=jnp.int32)[:, None]
    col_index = jnp.arange(length, dtype=jnp.int32)[None, :]
    angles = 2.0 * math.pi / length * (row_index * col_index % length).astype(jnp.float32)
    cosine = jnp.cos(angles)
    sine_part = jnp.sin(angles)
    return jnp.stack([jnp.stack([cosine, -sine_part], 1), jnp.stack([sine_part, cosine], 1)], 0)


def frame_table():
    frames = jnp.arange(TDFT, dtype=jnp.int32)[:, None]
    freqs = jnp.arange(1, MODF + 1, dtype=jnp.int32)[None, :]
    angles = 2.0 * math.pi / TDFT * (frames * freqs % TDFT).astype(jnp.float32)
    return jnp.concatenate([jnp.cos(angles), -jnp.sin(angles)], 1) / math.sqrt(TDFT)


def form_beams(transposed_block, feed_gains, cell_feed):
    chan_count = transposed_block.shape[1]
    pol_count = transposed_block.shape[2]
    values = transposed_block.reshape(2, chan_count, pol_count, FEEDS, TDFT).astype(jnp.float32)
    gain_values = feed_gains.astype(jnp.float32)[:, :, None, :, None]
    real_part = gain_values[0] * values[0] - gain_values[1] * values[1]
    imag_part = gain_values[0] * values[1] + gain_values[1] * values[0]
    calibrated = jnp.stack([real_part, imag_part]).astype(jnp.bfloat16)
    gridded = jnp.take(calibrated, cell_feed, axis=3).reshape(
        2, chan_count, pol_count, GRID_X, GRID_Y, TDFT
    )
    rows = twiddle_table(GRID_Y).astype(jnp.bfloat16)
    row_beams = jnp.einsum("acpxyn,aybw->bcpxwn", gridded, rows, preferred_element_type=jnp.float32)
    beam_voltage = jnp.einsum(
        "bcpxwn,bxeu->ecpnuw", row_beams, twiddle_table(GRID_X), precision=lax.Precision.HIGHEST
    )
    powers = jnp.sum(beam_voltage * beam_voltage, axis=0)
    return jnp.moveaxis(powers, 1, 0).reshape(pol_count, chan_count, TDFT, FEEDS)


def dedisperse(freq_major, delays):
    residues = delays % TDFT
    contract = (((0,), (0,)), ((), ()))

    def per_frequency(position_index):
        frequency = position_index + 1
        angles = 2.0 * math.pi / TDFT * (frequency * residues % TDFT).astype(jnp.float32)
        cosine_part = jnp.cos(angles).astype(jnp.bfloat16)
        sine_part = jnp.sin(angles).astype(jnp.bfloat16)
        mod_real = freq_major[position_index]
        mod_imag = freq_major[MODF + position_index]
        real_out = lax.dot_general(
            cosine_part, mod_real, contract, preferred_element_type=jnp.float32
        ) + lax.dot_general(sine_part, mod_imag, contract, preferred_element_type=jnp.float32)
        imag_out = lax.dot_general(
            cosine_part, mod_imag, contract, preferred_element_type=jnp.float32
        ) - lax.dot_general(sine_part, mod_real, contract, preferred_element_type=jnp.float32)
        result = jnp.stack([real_out, imag_out], 1) / math.sqrt(CHANS)
        return result.astype(jnp.bfloat16)

    return lax.map(per_frequency, jnp.arange(MODF, dtype=jnp.int32))


def combine(earlier, later):
    return (
        earlier[0] * later[0],
        later[0] * earlier[1] + later[1],
        later[0] * earlier[2] + later[2],
    )


def shards(voltages, feed_gains, grid_index, decay_rates, delays):
    cell_feed = (
        jnp.zeros((FEEDS,), jnp.int32).at[grid_index].set(jnp.arange(FEEDS, dtype=jnp.int32))
    )
    local_feeds = voltages.shape[2]
    samples = voltages[0].reshape(POL * local_feeds * TDFT, NSAMP)
    spectra = lax.dot_general(
        spectral_constant(), samples, (((1,), (1,)), ((), ())), preferred_element_type=jnp.float32
    )
    spectra = (
        (spectra * (1.0 / math.sqrt(NSAMP)))
        .astype(jnp.bfloat16)
        .reshape(2, CHANS, POL, local_feeds * TDFT)
    )
    turned = lax.all_to_all(spectra, "shard", split_axis=1, concat_axis=3, tiled=True)
    per_pol = form_beams(turned, feed_gains, cell_feed)
    beam_power = jnp.sum(per_pol, axis=0)
    levels = jnp.mean(beam_power, axis=(1, 2)) + 1e-06
    unity = jnp.ones_like(levels)
    nothing = jnp.zeros_like(levels)
    prefix = carried_in((decay_rates, levels, unity), "section", combine, (unity, nothing, nothing))
    baseline_level = (decay_rates * prefix[1] + levels) / (decay_rates * prefix[2] + 1.0)
    normalized = beam_power / baseline_level[:, None, None] - 1.0
    modulated = jnp.einsum(
        "cnb,nq->cbq", normalized, frame_table(), precision=lax.Precision.HIGHEST
    ).astype(jnp.bfloat16)
    flattened = modulated.reshape(modulated.shape[0], FEEDS * 2 * MODF)
    moved = lax.all_to_all(flattened, "shard", split_axis=1, concat_axis=0, tiled=True)
    local_beams = FEEDS // lax.axis_size("shard")
    gathered = moved.reshape(CHANS, local_beams, 2 * MODF)
    freq_major = jnp.transpose(gathered, (2, 0, 1))
    return dedisperse(freq_major, delays)[None]


def solution(mesh):
    in_specs = (P("section", None, "shard", None), P(None, "shard", None), P(), P("shard"), P())
    out_specs = P("section", None, None, None, "shard")
    return jax.shard_map(shards, mesh=mesh, in_specs=in_specs, out_specs=out_specs, check_vma=False)
```

profile of v0, /device:TPU:1, one launch (start us, length us, event | category | flops | bytes accessed | tf_op | source)
XLA Modules:
  0.0 509.8 jit_solution(17534313984835223672)
XLA Ops:
  0.0 2.9 reshape_squeeze.3
  2.9 9.2 %multiply_convert_fusion = bf16[2048,512]{1,0:T(8,128)(2,1)} fusion(bf16[2048,2048]{1,0:T(8,128)(2,1)} %constant.189, bf16[512,2048]{1,0:T(8,128)(2,1)S(1)} %reshape_squeeze.3), kind=kOutput, calls=%fused_computation.43 | convolution fusion | flops 4297064448 | bytes 12582912 | tf_op jit(solution)/shard_map/dot_general | solution.py:113
  12.1 2.5 reshape.245
  14.6 2.8 copy.40
  17.4 13.3 %all-to-all-start = ((bf16[2,1024,2,256]{3,2,0,1:T(2,128)(2,1)}), bf16[2,1024,2,256]{3,2,0,1:T(2,128)(2,1)S(1)}, u32[]{:S(2)}, u32[]{:S(2)}) async-start(bf16[2,1024,2,256]{3,2,0,1:T(2,128)(2,1)} %copy.40), calls=%async_computation | async-start | bytes 4194304 | tf_op jit(solution)/shard_map/all_to_all | solution.py:121
  30.8 4.5 scatter_custom_fusion
  40.3 40.2 %all-to-all-done = bf16[2,1024,2,256]{3,2,0,1:T(2,128)(2,1)S(1)} async-done(((bf16[2,1024,2,256]{3,2,0,1:T(2,128)(2,1)}), bf16[2,1024,2,256]{3,2,0,1:T(2,128)(2,1)S(1)}, u32[]{:S(2)}, u32[]{:S(2)}) %all-to-all-start) | async-done | bytes 2097184 | tf_op jit(solution)/shard_map/all_to_all | solution.py:121
  81.3 2.0 fusion.76
  84.5 8.6 %slice.26 = f32[1,16,2,1024,16]{4,3,2,1,0:T(8,128)} reshape(f32[1,16,2,64,256]{4,3,2,1,0:T(8,128)S(1)} %copy.42) | data formatting | bytes 4194304 | tf_op jit(solution)/shard_map/slice | solution.py:61
  93.1 2.8 copy.43
  95.9 8.6 %slice.29 = f32[1,16,2,1024,16]{4,3,2,1,0:T(8,128)} reshape(f32[1,16,2,64,256]{4,3,2,1,0:T(8,128)S(1)} %copy.43) | data formatting | bytes 4194304 | tf_op jit(solution)/shard_map/slice | solution.py:61
  104.5 18.1 %multiply_subtract_fusion = (bf16[1,16,2,1024,16]{4,3,2,1,0:T(8,128)(2,1)}, bf16[1,16,2,1024,16]{4,3,2,1,0:T(8,128)(2,1)}) fusion(f32[1,16,2,1024,16]{4,3,2,1,0:T(8,128)} %slice.29, f32[1,16,2,1024,16]{4,3,2,1,0:T(8,128)} %slice.26, f32[16,1024]{1,0:T(8,128)S(1)} %get-tuple-element.203, f32[16,1024]{1,0:T(8,128)S(1)} %get-tuple-element.202), kind=kLoop, calls=%fused_computation.37 | loop fusion | flops 4194304 | bytes 6422528 | tf_op jit(solution)/shard_map/sub | solution.py:61
  122.5 6.7 %copy.44 = bf16[1,16,2,1024,16]{3,4,2,1,0:T(8,128)(2,1)S(1)} copy(bf16[1,16,2,1024,16]{4,3,2,1,0:T(8,128)(2,1)} %get-tuple-element.196) | data formatting | bytes 2097152 | tf_op jit(solution)/shard_map/sub | solution.py:61
  129.2 7.8 %copy.45 = bf16[1,16,2,1024,16]{3,4,2,1,0:T(8,128)(2,1)} copy(bf16[1,16,2,1024,16]{4,3,2,1,0:T(8,128)(2,1)} %get-tuple-element.197) | data formatting | bytes 2097152 | tf_op jit(solution)/shard_map/add | solution.py:62
  137.0 1.4 pad_maximum_fusion
  138.4 16.1 %copy.46 = bf16[2,16,2,1024,16]{4,1,3,2,0:T(8,128)(2,1)} copy(bf16[2,16,2,1024,16]{3,4,2,1,0:T(8,128)(2,1)S(1)} %pad_maximum_fusion) | data formatting | bytes 4194304 | tf_op jit(solution)/shard_map/stack | solution.py:63
  154.5 20.1 %gather_fusion = bf16[1024,2,16,2,16]{4,2,3,1,0:T(8,128)(2,1)} fusion(bf16[2,16,2,1024,16]{4,1,3,2,0:T(8,128)(2,1)} %copy.46, s32[1024]{0:T(1024)S(1)} %fusion.59), kind=kCustom, calls=%fused_computation | custom fusion | bytes 4198400 | tf_op jit(solution)/shard_map/jit(_take)/gather | solution.py:64
  174.7 17.1 %copy.47 = bf16[2,16,2,4,256,16]{4,5,0,3,2,1:T(8,128)(2,1)S(1)} copy(bf16[2,16,2,4,256,16]{5,1,2,0,4,3:T(8,128)(2,1)} %bitcast.111) | data formatting | bytes 4194304 | tf_op jit(solution)/shard_map/jit(_take)/gather | solution.py:64
  191.8 1.3 convolution_bitcast_fusion
  193.1 12.4 %fusion.25 = (f32[16]{0:T(128)S(1)}, f32[4,16,256,16]{2,0,3,1:T(4,128)S(1)}) fusion(f32[2,16,2,4,256,16]{4,5,3,2,1,0:T(8,128)S(1)} %convolution_bitcast_fusion, f32[1,4,2,4]{1,3,0,2:T(4,128)S(1)} %copy.38, f32[1,4,2,4]{1,3,0,2:T(4,128)S(1)} %copy.37), kind=kOutput, calls=%fused_computation.44 | convolution fusion | flops 103546928 | bytes 5243200 | tf_op jit(solution)/shard_map/bcpxwn,bxeu->ecpnuw/dot_general | solution.py:69
  205.6 8.4 %all-reduce.2 = (f32[64]{0:T(128)S(1)}, f32[64]{0:T(128)S(1)}) all-reduce(f32[64]{0:T(128)S(1)} %dynamic-update-slice, f32[64]{0:T(128)S(1)} %fusion.69), channel_id=2, replica_groups=mesh['section'=4,'shard'=64] {'section'}, use_global_device_ids=true, to_apply=%add | all-reduce | flops 128 | bytes 1024
  215.9 3.3 copy.49
  219.2 5.8 %all_to_all.20 = bf16[16,64,224]{2,1,0:T(8,128)(2,1)S(1)} reshape(bf16[16,1024,14]{2,1,0:T(8,128)(2,1)} %copy.49) | data formatting | bytes 917504 | tf_op jit(solution)/shard_map/all_to_all | solution.py:134
  226.1 9.0 %all-to-all-start.1 = ((bf16[16,64,224]{2,0,1:T(8,128)(2,1)}), bf16[16,64,224]{2,0,1:T(8,128)(2,1)S(1)}, u32[]{:S(2)}, u32[]{:S(2)}) async-start(bf16[16,64,224]{2,0,1:T(8,128)(2,1)} %copy.50), calls=%async_computation.1 | async-start | bytes 1048576 | tf_op jit(solution)/shard_map/all_to_all | solution.py:134
  235.1 2.1 add_select_fusion.1
  237.2 15.6 %all-to-all-done.1 = bf16[16,64,224]{2,0,1:T(8,128)(2,1)S(1)} async-done(((bf16[16,64,224]{2,0,1:T(8,128)(2,1)}), bf16[16,64,224]{2,0,1:T(8,128)(2,1)S(1)}, u32[]{:S(2)}, u32[]{:S(2)}) %all-to-all-start.1) | async-done | bytes 458784 | tf_op jit(solution)/shard_map/all_to_all | solution.py:134
  252.8 3.3 copy.51
  256.1 6.7 %reshape.246 = bf16[1024,16,14]{0,2,1:T(8,128)(2,1)S(1)} reshape(bf16[64,16,224]{1,0,2:T(8,128)(2,1)} %copy.51) | data formatting | bytes 917504 | tf_op jit(solution)/shard_map/reshape | solution.py:136
  263.1 246.5 %while.28 = (s32[]{:T(128)}, bf16[7,512,2,16]{1,3,2,0:T(8,128)(2,1)}, s32[7]{0:T(128)S(1)}, s32[1024,512]{1,0:T(8,128)}, bf16[14,1024,16]{1,2,0:T(8,128)(2,1)S(1...) while((s32[]{:T(128)}, bf16[7,512,2,16]{1,3,2,0:T(8,128)(2,1)}, s32[7]{0:T(128)S(1)}, ...), condition=%wide.region_6.7_spmd, body=%wide.region_5.6_spmd.sunk | while | flops 76611592 | bytes 13009633 | solution.py:96
  266.4 2.5 fusion.95
  269.0 6.9 %fusion.98 = f32[512,16]{0,1:T(8,128)S(1)} fusion(f32[1024,512]{1,0:T(8,128)S(1)} %fusion.95, bf16[14,1024,16]{1,2,0:T(8,128)(2,1)S(1)} %get-tuple-element.336, s32[]{:T(128)S(6)} %select_n.175), kind=kOutput, calls=%fused_computation.19.clone.1 | convolution fusion | flops 17301504 | bytes 2162692 | tf_op jit(solution)/shard_map/while/body/eval_jaxpr/dot_general | solution.py:87
  277.1 6.9 %fusion.99 = f32[1,512,1,16]{1,3,2,0:T(8,128)S(1)} fusion(f32[512,16]{0,1:T(8,128)S(1)} %fusion.98, f32[1024,512]{1,0:T(8,128)S(1)} %fusion.95, bf16[14,1024,16]{1,2,0:T(8,128)(2,1)S(1)} %get-tuple-element.336, s32[]{:T(128)S(6)} %select_n.174), kind=kOutput, calls=%fused_computation.18.clone.1 | convolution fusion | flops 17309696 | bytes 2195460 | tf_op jit(solution)/shard_map/while/body/eval_jaxpr/dot_general | solution.py:89
  284.1 6.9 %fusion.96 = f32[512,16]{0,1:T(8,128)S(1)} fusion(f32[1024,512]{1,0:T(8,128)S(1)} %fusion.95, bf16[14,1024,16]{1,2,0:T(8,128)(2,1)S(1)} %get-tuple-element.336, s32[]{:T(128)S(6)} %select_n.174), kind=kOutput, calls=%fused_computation.20.clone.1 | convolution fusion | flops 17301504 | bytes 2162692 | tf_op jit(solution)/shard_map/while/body/eval_jaxpr/dot_general | solution.py:90
  290.9 6.9 %fusion.97 = f32[1,512,1,16]{1,3,2,0:T(8,128)S(1)} fusion(f32[512,16]{0,1:T(8,128)S(1)} %fusion.96, f32[1024,512]{1,0:T(8,128)S(1)} %fusion.95, bf16[14,1024,16]{1,2,0:T(8,128)(2,1)S(1)} %get-tuple-element.336, s32[]{:T(128)S(6)} %select_n.175), kind=kOutput, calls=%fused_computation.16.clone.1 | convolution fusion | flops 17309696 | bytes 2195460 | tf_op jit(solution)/shard_map/while/body/eval_jaxpr/dot_general | solution.py:92
  301.6 2.5 fusion.95
  304.2 6.9 %fusion.98 = f32[512,16]{0,1:T(8,128)S(1)} fusion(f32[1024,512]{1,0:T(8,128)S(1)} %fusion.95, bf16[14,1024,16]{1,2,0:T(8,128)(2,1)S(1)} %get-tuple-element.336, s32[]{:T(128)S(6)} %select_n.175), kind=kOutput, calls=%fused_computation.19.clone.1 | convolution fusion | flops 17301504 | bytes 2162692 | tf_op jit(solution)/shard_map/while/body/eval_jaxpr/dot_general | solution.py:87
  312.3 6.9 %fusion.99 = f32[1,512,1,16]{1,3,2,0:T(8,128)S(1)} fusion(f32[512,16]{0,1:T(8,128)S(1)} %fusion.98, f32[1024,512]{1,0:T(8,128)S(1)} %fusion.95, bf16[14,1024,16]{1,2,0:T(8,128)(2,1)S(1)} %get-tuple-element.336, s32[]{:T(128)S(6)} %select_n.174), kind=kOutput, calls=%fused_computation.18.clone.1 | convolution fusion | flops 17309696 | bytes 2195460 | tf_op jit(solution)/shard_map/while/body/eval_jaxpr/dot_general | solution.py:89
  319.3 6.9 %fusion.96 = f32[512,16]{0,1:T(8,128)S(1)} fusion(f32[1024,512]{1,0:T(8,128)S(1)} %fusion.95, bf16[14,1024,16]{1,2,0:T(8,128)(2,1)S(1)} %get-tuple-element.336, s32[]{:T(128)S(6)} %select_n.174), kind=kOutput, calls=%fused_computation.20.clone.1 | convolution fusion | flops 17301504 | bytes 2162692 | tf_op jit(solution)/shard_map/while/body/eval_jaxpr/dot_general | solution.py:90
  326.1 6.9 %fusion.97 = f32[1,512,1,16]{1,3,2,0:T(8,128)S(1)} fusion(f32[512,16]{0,1:T(8,128)S(1)} %fusion.96, f32[1024,512]{1,0:T(8,128)S(1)} %fusion.95, bf16[14,1024,16]{1,2,0:T(8,128)(2,1)S(1)} %get-tuple-element.336, s32[]{:T(128)S(6)} %select_n.175), kind=kOutput, calls=%fused_computation.16.clone.1 | convolution fusion | flops 17309696 | bytes 2195460 | tf_op jit(solution)/shard_map/while/body/eval_jaxpr/dot_general | solution.py:92
  336.8 2.5 fusion.95
  339.4 6.9 %fusion.98 = f32[512,16]{0,1:T(8,128)S(1)} fusion(f32[1024,512]{1,0:T(8,128)S(1)} %fusion.95, bf16[14,1024,16]{1,2,0:T(8,128)(2,1)S(1)} %get-tuple-element.336, s32[]{:T(128)S(6)} %select_n.175), kind=kOutput, calls=%fused_computation.19.clone.1 | convolution fusion | flops 17301504 | bytes 2162692 | tf_op jit(solution)/shard_map/while/body/eval_jaxpr/dot_general | solution.py:87
  347.5 6.9 %fusion.99 = f32[1,512,1,16]{1,3,2,0:T(8,128)S(1)} fusion(f32[512,16]{0,1:T(8,128)S(1)} %fusion.98, f32[1024,512]{1,0:T(8,128)S(1)} %fusion.95, bf16[14,1024,16]{1,2,0:T(8,128)(2,1)S(1)} %get-tuple-element.336, s32[]{:T(128)S(6)} %select_n.174), kind=kOutput, calls=%fused_computation.18.clone.1 | convolution fusion | flops 17309696 | bytes 2195460 | tf_op jit(solution)/shard_map/while/body/eval_jaxpr/dot_general | solution.py:89
  354.4 6.9 %fusion.96 = f32[512,16]{0,1:T(8,128)S(1)} fusion(f32[1024,512]{1,0:T(8,128)S(1)} %fusion.95, bf16[14,1024,16]{1,2,0:T(8,128)(2,1)S(1)} %get-tuple-element.336, s32[]{:T(128)S(6)} %select_n.174), kind=kOutput, calls=%fused_computation.20.clone.1 | convolution fusion | flops 17301504 | bytes 2162692 | tf_op jit(solution)/shard_map/while/body/eval_jaxpr/dot_general | solution.py:90
  361.3 6.9 %fusion.97 = f32[1,512,1,16]{1,3,2,0:T(8,128)S(1)} fusion(f32[512,16]{0,1:T(8,128)S(1)} %fusion.96, f32[1024,512]{1,0:T(8,128)S(1)} %fusion.95, bf16[14,1024,16]{1,2,0:T(8,128)(2,1)S(1)} %get-tuple-element.336, s32[]{:T(128)S(6)} %select_n.175), kind=kOutput, calls=%fused_computation.16.clone.1 | convolution fusion | flops 17309696 | bytes 2195460 | tf_op jit(solution)/shard_map/while/body/eval_jaxpr/dot_general | solution.py:92
  372.0 2.5 fusion.95
  374.5 6.9 %fusion.98 = f32[512,16]{0,1:T(8,128)S(1)} fusion(f32[1024,512]{1,0:T(8,128)S(1)} %fusion.95, bf16[14,1024,16]{1,2,0:T(8,128)(2,1)S(1)} %get-tuple-element.336, s32[]{:T(128)S(6)} %select_n.175), kind=kOutput, calls=%fused_computation.19.clone.1 | convolution fusion | flops 17301504 | bytes 2162692 | tf_op jit(solution)/shard_map/while/body/eval_jaxpr/dot_general | solution.py:87
  382.7 6.9 %fusion.99 = f32[1,512,1,16]{1,3,2,0:T(8,128)S(1)} fusion(f32[512,16]{0,1:T(8,128)S(1)} %fusion.98, f32[1024,512]{1,0:T(8,128)S(1)} %fusion.95, bf16[14,1024,16]{1,2,0:T(8,128)(2,1)S(1)} %get-tuple-element.336, s32[]{:T(128)S(6)} %select_n.174), kind=kOutput, calls=%fused_computation.18.clone.1 | convolution fusion | flops 17309696 | bytes 2195460 | tf_op jit(solution)/shard_map/while/body/eval_jaxpr/dot_general | solution.py:89
  389.6 6.9 %fusion.96 = f32[512,16]{0,1:T(8,128)S(1)} fusion(f32[1024,512]{1,0:T(8,128)S(1)} %fusion.95, bf16[14,1024,16]{1,2,0:T(8,128)(2,1)S(1)} %get-tuple-element.336, s32[]{:T(128)S(6)} %select_n.174), kind=kOutput, calls=%fused_computation.20.clone.1 | convolution fusion | flops 17301504 | bytes 2162692 | tf_op jit(solution)/shard_map/while/body/eval_jaxpr/dot_general | solution.py:90
  396.5 6.9 %fusion.97 = f32[1,512,1,16]{1,3,2,0:T(8,128)S(1)} fusion(f32[512,16]{0,1:T(8,128)S(1)} %fusion.96, f32[1024,512]{1,0:T(8,128)S(1)} %fusion.95, bf16[14,1024,16]{1,2,0:T(8,128)(2,1)S(1)} %get-tuple-element.336, s32[]{:T(128)S(6)} %select_n.175), kind=kOutput, calls=%fused_computation.16.clone.1 | convolution fusion | flops 17309696 | bytes 2195460 | tf_op jit(solution)/shard_map/while/body/eval_jaxpr/dot_general | solution.py:92
  407.2 2.5 fusion.95
  409.7 6.9 %fusion.98 = f32[512,16]{0,1:T(8,128)S(1)} fusion(f32[1024,512]{1,0:T(8,128)S(1)} %fusion.95, bf16[14,1024,16]{1,2,0:T(8,128)(2,1)S(1)} %get-tuple-element.336, s32[]{:T(128)S(6)} %select_n.175), kind=kOutput, calls=%fused_computation.19.clone.1 | convolution fusion | flops 17301504 | bytes 2162692 | tf_op jit(solution)/shard_map/while/body/eval_jaxpr/dot_general | solution.py:87
  417.9 6.9 %fusion.99 = f32[1,512,1,16]{1,3,2,0:T(8,128)S(1)} fusion(f32[512,16]{0,1:T(8,128)S(1)} %fusion.98, f32[1024,512]{1,0:T(8,128)S(1)} %fusion.95, bf16[14,1024,16]{1,2,0:T(8,128)(2,1)S(1)} %get-tuple-element.336, s32[]{:T(128)S(6)} %select_n.174), kind=kOutput, calls=%fused_computation.18.clone.1 | convolution fusion | flops 17309696 | bytes 2195460 | tf_op jit(solution)/shard_map/while/body/eval_jaxpr/dot_general | solution.py:89
  424.8 6.9 %fusion.96 = f32[512,16]{0,1:T(8,128)S(1)} fusion(f32[1024,512]{1,0:T(8,128)S(1)} %fusion.95, bf16[14,1024,16]{1,2,0:T(8,128)(2,1)S(1)} %get-tuple-element.336, s32[]{:T(128)S(6)} %select_n.174), kind=kOutput, calls=%fused_computation.20.clone.1 | convolution fusion | flops 17301504 | bytes 2162692 | tf_op jit(solution)/shard_map/while/body/eval_jaxpr/dot_general | solution.py:90
  431.7 6.9 %fusion.97 = f32[1,512,1,16]{1,3,2,0:T(8,128)S(1)} fusion(f32[512,16]{0,1:T(8,128)S(1)} %fusion.96, f32[1024,512]{1,0:T(8,128)S(1)} %fusion.95, bf16[14,1024,16]{1,2,0:T(8,128)(2,1)S(1)} %get-tuple-element.336, s32[]{:T(128)S(6)} %select_n.175), kind=kOutput, calls=%fused_computation.16.clone.1 | convolution fusion | flops 17309696 | bytes 2195460 | tf_op jit(solution)/shard_map/while/body/eval_jaxpr/dot_general | solution.py:92
  442.4 2.5 fusion.95
  444.9 6.9 %fusion.98 = f32[512,16]{0,1:T(8,128)S(1)} fusion(f32[1024,512]{1,0:T(8,128)S(1)} %fusion.95, bf16[14,1024,16]{1,2,0:T(8,128)(2,1)S(1)} %get-tuple-element.336, s32[]{:T(128)S(6)} %select_n.175), kind=kOutput, calls=%fused_computation.19.clone.1 | convolution fusion | flops 17301504 | bytes 2162692 | tf_op jit(solution)/shard_map/while/body/eval_jaxpr/dot_general | solution.py:87
  453.1 6.9 %fusion.99 = f32[1,512,1,16]{1,3,2,0:T(8,128)S(1)} fusion(f32[512,16]{0,1:T(8,128)S(1)} %fusion.98, f32[1024,512]{1,0:T(8,128)S(1)} %fusion.95, bf16[14,1024,16]{1,2,0:T(8,128)(2,1)S(1)} %get-tuple-element.336, s32[]{:T(128)S(6)} %select_n.174), kind=kOutput, calls=%fused_computation.18.clone.1 | convolution fusion | flops 17309696 | bytes 2195460 | tf_op jit(solution)/shard_map/while/body/eval_jaxpr/dot_general | solution.py:89
  460.0 6.9 %fusion.96 = f32[512,16]{0,1:T(8,128)S(1)} fusion(f32[1024,512]{1,0:T(8,128)S(1)} %fusion.95, bf16[14,1024,16]{1,2,0:T(8,128)(2,1)S(1)} %get-tuple-element.336, s32[]{:T(128)S(6)} %select_n.174), kind=kOutput, calls=%fused_computation.20.clone.1 | convolution fusion | flops 17301504 | bytes 2162692 | tf_op jit(solution)/shard_map/while/body/eval_jaxpr/dot_general | solution.py:90
  466.9 6.9 %fusion.97 = f32[1,512,1,16]{1,3,2,0:T(8,128)S(1)} fusion(f32[512,16]{0,1:T(8,128)S(1)} %fusion.96, f32[1024,512]{1,0:T(8,128)S(1)} %fusion.95, bf16[14,1024,16]{1,2,0:T(8,128)(2,1)S(1)} %get-tuple-element.336, s32[]{:T(128)S(6)} %select_n.175), kind=kOutput, calls=%fused_computation.16.clone.1 | convolution fusion | flops 17309696 | bytes 2195460 | tf_op jit(solution)/shard_map/while/body/eval_jaxpr/dot_general | solution.py:92
  477.6 2.5 fusion.95
  480.1 6.9 %fusion.98 = f32[512,16]{0,1:T(8,128)S(1)} fusion(f32[1024,512]{1,0:T(8,128)S(1)} %fusion.95, bf16[14,1024,16]{1,2,0:T(8,128)(2,1)S(1)} %get-tuple-element.336, s32[]{:T(128)S(6)} %select_n.175), kind=kOutput, calls=%fused_computation.19.clone.1 | convolution fusion | flops 17301504 | bytes 2162692 | tf_op jit(solution)/shard_map/while/body/eval_jaxpr/dot_general | solution.py:87
  488.3 6.9 %fusion.99 = f32[1,512,1,16]{1,3,2,0:T(8,128)S(1)} fusion(f32[512,16]{0,1:T(8,128)S(1)} %fusion.98, f32[1024,512]{1,0:T(8,128)S(1)} %fusion.95, bf16[14,1024,16]{1,2,0:T(8,128)(2,1)S(1)} %get-tuple-element.336, s32[]{:T(128)S(6)} %select_n.174), kind=kOutput, calls=%fused_computation.18.clone.1 | convolution fusion | flops 17309696 | bytes 2195460 | tf_op jit(solution)/shard_map/while/body/eval_jaxpr/dot_general | solution.py:89
  495.2 6.9 %fusion.96 = f32[512,16]{0,1:T(8,128)S(1)} fusion(f32[1024,512]{1,0:T(8,128)S(1)} %fusion.95, bf16[14,1024,16]{1,2,0:T(8,128)(2,1)S(1)} %get-tuple-element.336, s32[]{:T(128)S(6)} %select_n.174), kind=kOutput, calls=%fused_computation.20.clone.1 | convolution fusion | flops 17301504 | bytes 2162692 | tf_op jit(solution)/shard_map/while/body/eval_jaxpr/dot_general | solution.py:90
  502.1 6.9 %fusion.97 = f32[1,512,1,16]{1,3,2,0:T(8,128)S(1)} fusion(f32[512,16]{0,1:T(8,128)S(1)} %fusion.96, f32[1024,512]{1,0:T(8,128)S(1)} %fusion.95, bf16[14,1024,16]{1,2,0:T(8,128)(2,1)S(1)} %get-tuple-element.336, s32[]{:T(128)S(6)} %select_n.175), kind=kOutput, calls=%fused_computation.16.clone.1 | convolution fusion | flops 17309696 | bytes 2195460 | tf_op jit(solution)/shard_map/while/body/eval_jaxpr/dot_general | solution.py:92
  (63 shorter events, 18.3 us)
Async XLA Ops:
  17.4 13.3 %copy-start.2 = (bf16[2,16,1024]{2,1,0:T(8,128)(2,1)S(1)}, bf16[2,16,1024]{2,1,0:T(8,128)(2,1)}, u32[]{:S(2)}) copy-start(bf16[2,16,1024]{2,1,0:T(8,128)(2,1)} %param.11) | copy-start | bytes 196612
  17.4 13.3 %copy-start.3 = (s32[1024]{0:T(1024)S(1)}, s32[1024]{0:T(1024)}, u32[]{:S(2)}) copy-start(s32[1024]{0:T(1024)} %param.12) | copy-start | bytes 12292
  17.4 18.3 %copy-start.5 = (u32[256]{0:T(256)S(1)}, u32[256]{0:T(256)}, u32[]{:S(2)}) copy-start(u32[256]{0:T(256)} %constant.192) | copy-start | bytes 3076
  17.4 19.6 %copy-start.4 = (f32[16]{0:T(128)S(1)}, f32[16]{0:T(128)}, u32[]{:S(2)}) copy-start(f32[16]{0:T(128)} %param.13) | copy-start | bytes 196
  17.4 63.0 %all-to-all-start = ((bf16[2,1024,2,256]{3,2,0,1:T(2,128)(2,1)}), bf16[2,1024,2,256]{3,2,0,1:T(2,128)(2,1)S(1)}, u32[]{:S(2)}, u32[]{:S(2)}) async-start(bf16[2,1024,2,256]{3,2,0,1:T(2,128)(2,1)} %copy.40), calls=%async_computation | async-start | bytes 4194304 | tf_op jit(solution)/shard_map/all_to_all | solution.py:121
  174.7 17.1 %copy-start.1 = (bf16[1,256,2,256]{3,1,0,2:T(8,128)(2,1)S(1)}, bf16[1,256,2,256]{3,1,0,2:T(8,128)(2,1)}, u32[]{:S(2)}) copy-start(bf16[1,256,2,256]{3,1,0,2:T(8,128)(2,1)} %get-tuple-element.201) | copy-start | bytes 786436
  225.0 10.1 %copy-start = (s32[1024,512]{1,0:T(8,128)S(1)}, s32[1024,512]{1,0:T(8,128)}, u32[]{:S(2)}) copy-start(s32[1024,512]{1,0:T(8,128)} %param.14) | copy-start | bytes 6291460
  226.1 26.7 %all-to-all-start.1 = ((bf16[16,64,224]{2,0,1:T(8,128)(2,1)}), bf16[16,64,224]{2,0,1:T(8,128)(2,1)S(1)}, u32[]{:S(2)}, u32[]{:S(2)}) async-start(bf16[16,64,224]{2,0,1:T(8,128)(2,1)} %copy.50), calls=%async_computation.1 | async-start | bytes 1048576 | tf_op jit(solution)/shard_map/all_to_all | solution.py:134
where the time goes:
time: 516 us; the launch traced here: 510 us
  matrix products  217 us (42%)
  local copies, waits for them, and re-layouts  131 us (25%)
  waiting for transfers between devices  55.8 us (11%)
  other arithmetic  47.6 us (9%)
  loops' own time  27.1 us (5%)
  starting transfers between devices  22.3 us (4%)
  blocking collectives  8.44 us (2%)
    dot_general x7, matrix products, per_frequency(): lax.dot_general(sine_part, mod_imag, contract, preferred_element_type=jnp...  48.5 us
    dot_general x7, matrix products, per_frequency(): lax.dot_general(sine_part, mod_real, contract, preferred_element_type=jnp...  48.4 us
    dot_general x7, matrix products, per_frequency(): lax.dot_general(cosine_part, mod_real, contract, preferred_element_type=j...  48.1 us
    dot_general x7, matrix products, per_frequency(): lax.dot_general(cosine_part, mod_imag, contract, preferred_element_type=j...  48 us
    all_to_all x1, waiting for transfers between devices, shards(): lax.all_to_all(spectra, 'shard', split_axis=1, concat_axis=3, tiled=True)  40.2 us
    gather x2, local copies, waits for them, and re-layouts, form_beams(): jnp.take(calibrated, cell_feed, axis=3)  37.3 us
    another operation x1, loops' own time, dedisperse(): return lax.map(per_frequency, jnp.arange(MODF, dtype=jnp.int32))  27.1 us
    slice x5, local copies, waits for them, and re-layouts, form_beams(): real_part = gain_values[0] * values[0] - gain_values[1] * values[1]  23.2 us
  transfers between devices with their start and end apart: 2, of which 2 were waited for; matrix products, arithmetic and copies ran while one was open for 2% of the time, Pallas kernels for 0%

commit v1 on v0

v1 whole, which is shorter than its diff:
```python
import math

import jax
import jax.numpy as jnp
import numpy as np
from jax import lax
from jax.experimental import pallas as pl
from jax.experimental.pallas import tpu as pltpu
from jax.sharding import PartitionSpec as P

POL = 2
GRID_X = 4
GRID_Y = 256
NSAMP = 2048
TDFT = 16
TRIALS = 512
FEEDS = 1024
CHANS = 1024
MODF = 7
BLOCKS = 4
SHARDS = 64
LOCAL = 16
VMEM_LIMIT = 56 * 1024 * 1024


def spectral_constant():
    dest, part, chan = np.meshgrid(np.arange(SHARDS), np.arange(2), np.arange(LOCAL), indexing="ij")
    chans = (dest * LOCAL + chan).reshape(-1).astype(np.int64)
    part = part.reshape(-1)
    cols = np.arange(NSAMP, dtype=np.int64)[None, :]
    angles = np.float32(2.0 * math.pi / NSAMP) * (chans[:, None] * cols % NSAMP).astype(np.float32)
    table = np.where(part[:, None] == 0, np.cos(angles), -np.sin(angles)).astype(np.float32)
    return jnp.asarray(table).astype(jnp.bfloat16)


def row_constant():
    rows = np.arange(GRID_Y)[:, None]
    cols = np.arange(GRID_Y)[None, :]
    angles = np.float32(2.0 * math.pi / GRID_Y) * (rows * cols % GRID_Y).astype(np.float32)
    table = np.concatenate([np.cos(angles), np.sin(angles)], 1).astype(np.float32)
    return jnp.asarray(table).astype(jnp.bfloat16)


def frame_matrix():
    frames = np.arange(TDFT)[:, None]
    freqs = np.arange(1, MODF + 1)[None, :]
    angles = 2.0 * math.pi / TDFT * (frames * freqs % TDFT)
    return np.concatenate([np.cos(angles), -np.sin(angles)], 1) / math.sqrt(TDFT)


def channelize_body(table_ref, volts_ref, out_ref, rows_ref):
    @pl.when(pl.program_id(0) == 0)
    def _():
        for pol in range(POL):
            for frame in range(TDFT):
                start = (pol * TDFT + frame) * LOCAL
                rows_ref[start : start + LOCAL, :] = volts_ref[
                    pol, :, frame * NSAMP : (frame + 1) * NSAMP
                ]

    spectra = lax.dot_general(
        table_ref[...], rows_ref[...], (((1,), (1,)), ((), ())), preferred_element_type=jnp.float32
    )
    out_ref[...] = (spectra * (1.0 / math.sqrt(NSAMP))).astype(jnp.bfloat16)


def channelize(volts):
    block = 256
    lanes = POL * TDFT * LOCAL
    return pl.pallas_call(
        channelize_body,
        out_shape=jax.ShapeDtypeStruct((2 * CHANS, lanes), jnp.bfloat16),
        grid=(2 * CHANS // block,),
        in_specs=[
            pl.BlockSpec((block, NSAMP), lambda i: (i, 0)),
            pl.BlockSpec((POL, LOCAL, TDFT * NSAMP), lambda i: (0, 0, 0)),
        ],
        out_specs=pl.BlockSpec((block, lanes), lambda i: (i, 0)),
        scratch_shapes=[pltpu.VMEM((lanes, NSAMP), jnp.bfloat16)],
        compiler_params=pltpu.CompilerParams(vmem_limit_bytes=VMEM_LIMIT),
        name="channelize",
    )(spectral_constant(), volts)


def cosine_of(step):
    fold = jnp.abs(8 - step)
    out = jnp.full(step.shape, -math.cos(0.0), jnp.float32)
    for entry in range(1, 9):
        out = jnp.where(fold == entry, np.float32(-math.cos(2.0 * math.pi * entry / TDFT)), out)
    return out


def phase_body(delay_ref, out_ref):
    step = delay_ref[...] & (TDFT - 1)
    cos_one = cosine_of(step)
    sin_one = cosine_of((step + 12) & (TDFT - 1))
    twice = 2.0 * cos_one
    cos_now, sin_now = cos_one, sin_one
    cos_last, sin_last = jnp.ones_like(cos_one), jnp.zeros_like(cos_one)
    for f in range(MODF):
        out_ref[f, 0] = cos_now.astype(jnp.bfloat16)
        out_ref[f, 1] = sin_now.astype(jnp.bfloat16)
        cos_now, cos_last = twice * cos_now - cos_last, cos_now
        sin_now, sin_last = twice * sin_now - sin_last, sin_now


def phase_tables(delays):
    block = 64
    return pl.pallas_call(
        phase_body,
        out_shape=jax.ShapeDtypeStruct((MODF, 2, CHANS, TRIALS), jnp.bfloat16),
        grid=(CHANS // block,),
        in_specs=[pl.BlockSpec((block, TRIALS), lambda i: (i, 0))],
        out_specs=pl.BlockSpec((MODF, 2, block, TRIALS), lambda i: (0, 0, i, 0)),
        compiler_params=pltpu.CompilerParams(vmem_limit_bytes=VMEM_LIMIT),
        name="phases",
    )(delays)


def beam_table_body(cell_ref, rows_ref, out_ref):
    cell = cell_ref[...]
    x = cell // GRID_Y
    y = cell % GRID_Y
    hot = (lax.broadcasted_iota(jnp.int32, (cell.shape[0], GRID_Y), 1) == y).astype(jnp.float32)
    both = jnp.dot(
        hot.astype(jnp.bfloat16), rows_ref[...], preferred_element_type=jnp.float32
    )
    cos, sin = both[:, :GRID_Y], both[:, GRID_Y:]
    for u in range(GRID_X):
        turn = (u * x) & 3
        real = jnp.where(turn == 0, cos, jnp.where(turn == 1, -sin, jnp.where(turn == 2, -cos, sin)))
        imag = jnp.where(turn == 0, -sin, jnp.where(turn == 1, -cos, jnp.where(turn == 2, sin, cos)))
        out_ref[0, :, u * GRID_Y : (u + 1) * GRID_Y] = real.astype(jnp.bfloat16)
        out_ref[1, :, u * GRID_Y : (u + 1) * GRID_Y] = imag.astype(jnp.bfloat16)


def beam_table(grid_index):
    block = 256
    return pl.pallas_call(
        beam_table_body,
        out_shape=jax.ShapeDtypeStruct((2, FEEDS, FEEDS), jnp.bfloat16),
        grid=(FEEDS // block,),
        in_specs=[
            pl.BlockSpec((block, 1), lambda i: (i, 0)),
            pl.BlockSpec((GRID_Y, 2 * GRID_Y), lambda i: (0, 0)),
        ],
        out_specs=pl.BlockSpec((2, block, FEEDS), lambda i: (0, i, 0)),
        compiler_params=pltpu.CompilerParams(vmem_limit_bytes=VMEM_LIMIT),
        name="beam_table",
    )(grid_index.reshape(FEEDS, 1), row_constant())


def exchange(parts):
    parts = list(parts)
    lane = lax.broadcasted_iota(jnp.int32, parts[0].shape, 1)
    for bit in (4, 2, 1):
        upper = (lane & (bit * LOCAL)) != 0
        for i in range(8):
            if i & bit:
                continue
            low, high = parts[i], parts[i + bit]
            parts[i] = jnp.where(upper, pltpu.roll(high, bit * LOCAL, 1), low)
            parts[i + bit] = jnp.where(upper, high, pltpu.roll(low, 128 - bit * LOCAL, 1))
    return parts


def calibrate_body(data_ref, gain_ref, out_ref, level_ref, sum_ref):
    octet = pl.program_id(0)
    gain_real = gain_ref[0].astype(jnp.float32)
    gain_imag = gain_ref[1].astype(jnp.float32)

    def one(tile, total):
        lanes = pl.ds(pl.multiple_of(tile * 128, 128), 128)
        parts = [data_ref[s, :, lanes].astype(jnp.float32) for s in range(8)]
        parts = exchange(parts)
        for n, part in enumerate(parts):
            real, imag = part[:LOCAL], part[LOCAL:]
            cal_real = (gain_real * real - gain_imag * imag).astype(jnp.bfloat16)
            cal_imag = (gain_real * imag + gain_imag * real).astype(jnp.bfloat16)
            rows = pl.ds(pl.multiple_of(tile * 128 + n * LOCAL, LOCAL), LOCAL)
            out_ref[0, rows, :] = cal_real
            out_ref[1, rows, :] = cal_imag
            wide_real, wide_imag = cal_real.astype(jnp.float32), cal_imag.astype(jnp.float32)
            total = total + (wide_real * wide_real + wide_imag * wide_imag)
        return total

    total = lax.fori_loop(0, 4, one, jnp.zeros((LOCAL, 128), jnp.float32))

    @pl.when(octet == 0)
    def _():
        sum_ref[...] = jnp.zeros_like(sum_ref)

    sum_ref[...] += total

    @pl.when(octet == 7)
    def _():
        level = jnp.sum(sum_ref[...], axis=1, keepdims=True) * (1.0 / TDFT) + 1e-06
        level_ref[...] = jnp.broadcast_to(level, level_ref.shape)


def calibrate(turned, feed_gains):
    rows = POL * TDFT * LOCAL
    return pl.pallas_call(
        calibrate_body,
        out_shape=(
            jax.ShapeDtypeStruct((2, rows, FEEDS), jnp.bfloat16),
            jax.ShapeDtypeStruct((LOCAL, 128), jnp.float32),
        ),
        grid=(8,),
        in_specs=[
            pl.BlockSpec((8, 2 * LOCAL, rows), lambda i: (i, 0, 0)),
            pl.BlockSpec((2, LOCAL, 128), lambda i: (0, 0, i)),
        ],
        out_specs=(
            pl.BlockSpec((2, rows, 128), lambda i: (0, 0, i)),
            pl.BlockSpec((LOCAL, 128), lambda i: (0, 0)),
        ),
        scratch_shapes=[pltpu.VMEM((LOCAL, 128), jnp.float32)],
        compiler_params=pltpu.CompilerParams(vmem_limit_bytes=VMEM_LIMIT),
        name="calibrate",
    )(turned, feed_gains)


def frame_transform(power):
    half = TDFT // 2
    table = frame_matrix()
    plus = [power[n] + power[n + half] for n in range(half)]
    minus = [power[n] - power[n + half] for n in range(half)]
    out = []
    for q in range(2 * MODF):
        source = minus if (q % MODF + 1) % 2 else plus
        total = None
        for n in range(half):
            factor = float(table[n, q])
            if abs(factor) < 1e-12:
                continue
            term = source[n] * np.float32(factor)
            total = term if total is None else total + term
        out.append(total)
    return out


def beam_body(cal_ref, table_ref, scale_ref, out_ref, power_ref):
    half = POL * TDFT * LOCAL // 2
    cal_real, cal_imag = cal_ref[0], cal_ref[1]
    real_table, imag_table = table_ref[0], table_ref[1]

    def mul(a, b):
        return jnp.dot(a, b, preferred_element_type=jnp.float32)

    real = mul(cal_real, real_table) - mul(cal_imag, imag_table)
    imag = mul(cal_real, imag_table) + mul(cal_imag, real_table)
    power = real * real + imag * imag
    power_ref[...] = power[:half] + power[half:]
    offset = frame_matrix().sum(0)
    scale = scale_ref[...]
    for tile in range(power_ref.shape[1] // 128):
        lanes = slice(tile * 128, (tile + 1) * 128)
        frames = [power_ref[n * LOCAL : (n + 1) * LOCAL, lanes] for n in range(TDFT)]
        freqs = frame_transform(frames)
        freqs = [v * scale - np.float32(offset[q]) for q, v in enumerate(freqs)]
        freqs = freqs + [jnp.zeros_like(freqs[0])] * 2
        for group in range(2):
            for j, part in enumerate(exchange(freqs[group * 8 : group * 8 + 8])):
                out_ref[tile * 8 + j, :, group * 128 : (group + 1) * 128] = part.astype(jnp.bfloat16)


def form_beams(calibrated, table, scale):
    block = 256
    rows = POL * TDFT * LOCAL
    return pl.pallas_call(
        beam_body,
        out_shape=jax.ShapeDtypeStruct((SHARDS, LOCAL, 256), jnp.bfloat16),
        grid=(FEEDS // block,),
        in_specs=[
            pl.BlockSpec((2, rows, FEEDS), lambda i: (0, 0, 0)),
            pl.BlockSpec((2, FEEDS, block), lambda i: (0, 0, i)),
            pl.BlockSpec((LOCAL, 128), lambda i: (0, 0)),
        ],
        out_specs=pl.BlockSpec((block // LOCAL, LOCAL, 256), lambda i: (i, 0, 0)),
        scratch_shapes=[pltpu.VMEM((rows // 2, block), jnp.float32)],
        compiler_params=pltpu.CompilerParams(vmem_limit_bytes=VMEM_LIMIT),
        name="beams",
    )(calibrated, table, scale)


def dedisperse_body(data_ref, phase_ref, out_ref, turned_ref):
    f = pl.program_id(0)

    @pl.when(f == 0)
    def _():
        turned_ref[...] = data_ref[...].astype(jnp.float32).T.astype(jnp.bfloat16)

    real = turned_ref[pl.ds(pl.multiple_of(f * LOCAL, LOCAL), LOCAL), :]
    imag = turned_ref[pl.ds(pl.multiple_of((f + MODF) * LOCAL, LOCAL), LOCAL), :]
    with_cos = jnp.concatenate([real, imag], 0)
    with_sin = jnp.concatenate([imag, -real], 0)
    total = jnp.dot(with_cos, phase_ref[0, 0], preferred_element_type=jnp.float32)
    total = total + jnp.dot(with_sin, phase_ref[0, 1], preferred_element_type=jnp.float32)
    out_ref[0] = (total * (1.0 / math.sqrt(CHANS))).astype(jnp.bfloat16)


def dedisperse(data, phases):
    return pl.pallas_call(
        dedisperse_body,
        out_shape=jax.ShapeDtypeStruct((MODF, 2 * LOCAL, TRIALS), jnp.bfloat16),
        grid=(MODF,),
        in_specs=[
            pl.BlockSpec((CHANS, 256), lambda i: (0, 0)),
            pl.BlockSpec((1, 2, CHANS, TRIALS), lambda i: (i, 0, 0, 0)),
        ],
        out_specs=pl.BlockSpec((1, 2 * LOCAL, TRIALS), lambda i: (i, 0, 0)),
        scratch_shapes=[pltpu.VMEM((256, CHANS), jnp.bfloat16)],
        compiler_params=pltpu.CompilerParams(vmem_limit_bytes=VMEM_LIMIT),
        name="dedisperse",
    )(data, phases)


def shards(voltages, feed_gains, grid_index, decay_rates, delays):
    spectra = channelize(voltages[0]).reshape(SHARDS, 2 * LOCAL, POL * TDFT * LOCAL)
    turned = lax.all_to_all(spectra, "shard", split_axis=0, concat_axis=0, tiled=True)
    phases = phase_tables(delays)
    table = beam_table(grid_index)
    calibrated, levels = calibrate(turned, feed_gains)
    gathered = lax.all_gather(levels[:, 0], "section")
    place = lax.axis_index("section")
    dividend = jnp.zeros_like(decay_rates)
    divisor = jnp.zeros_like(decay_rates)
    for block in range(BLOCKS):
        use = block <= place
        dividend = jnp.where(use, decay_rates * dividend + gathered[block], dividend)
        divisor = jnp.where(use, decay_rates * divisor + 1.0, divisor)
    scale = jnp.broadcast_to((divisor / dividend)[:, None], (LOCAL, 128))
    modulated = form_beams(calibrated, table, scale)
    moved = lax.all_to_all(modulated, "shard", split_axis=0, concat_axis=0, tiled=True)
    out = dedisperse(moved.reshape(CHANS, 256), phases)
    return out.reshape(MODF, 2, LOCAL, TRIALS).transpose(0, 3, 1, 2)[None]


def solution(mesh):
    in_specs = (P("section", None, "shard", None), P(None, "shard", None), P(), P("shard"), P())
    out_specs = P("section", None, None, None, "shard")
    return jax.shard_map(shards, mesh=mesh, in_specs=in_specs, out_specs=out_specs, check_vma=False)
```

time: 516 us -> 143 us (0.28)
  matrix products: 217 us -> 0 us
  local copies, waits for them, and re-layouts: 131 us -> 5.52 us
  Pallas kernels: 0 us -> 58.3 us
  other arithmetic: 47.6 us -> 0.08 us
  loops' own time: 27.1 us -> 0 us
  waiting for transfers between devices: 55.8 us -> 46.1 us
    dot_general x32 -> x0, matrix products: 217 us -> none  [the longest x7 48.5 us: per_frequency(): lax.dot_general(sine_part, mod_imag, contract, preferred_element_type=jnp...]
    pallas_call x0 -> x6, Pallas kernels: none -> 58.3 us  [the longest x1 13.8 us: phase_tables(): pl.pallas_call(phase_body, out_shape=jax.ShapeDtypeStruct((MODF, 2, CHANS...]
    gather x2 -> x0, local copies, waits for them, and re-layouts: 37.3 us -> none  [form_beams(): jnp.take(calibrated, cell_feed, axis=3)]
    another operation x2 -> x0, loops' own time: 27.1 us -> none  [the longest x1 27.1 us: dedisperse(): return lax.map(per_frequency, jnp.arange(MODF, dtype=jnp.int32))]
    slice x5 -> x1, local copies, waits for them, and re-layouts: 23.2 us -> 0.81 us  [shards(): gathered = lax.all_gather(levels[:, 0], 'section')]
    another operation x6 -> x0, local copies, waits for them, and re-layouts: 19.2 us -> none  [the longest x1 16.1 us: form_beams(): calibrated = jnp.stack([real_part, imag_part]).astype(jnp.bfloat16)]
    sub x1 -> x0, other arithmetic: 18.1 us -> none  [form_beams(): real_part = gain_values[0] * values[0] - gain_values[1] * values[1]]
    mul x7 -> x0, other arithmetic: 17.8 us -> none  [per_frequency(): 2.0 * math.pi / TDFT * (frequency * residues % TDFT).astype(jnp.float32)]
  transfers between devices with their start and end apart: 2 -> 2, of which waited for: 2 -> 2; matrix products, arithmetic and copies ran while one was open for 2% -> 1% of each run, Pallas kernels for 0% -> 13%
where the time goes in v1:
time: 143 us; the launch traced here: 141 us
  Pallas kernels  58.3 us (41%)
  waiting for transfers between devices  46.1 us (32%)
  starting transfers between devices  22.3 us (16%)
  blocking collectives  8.43 us (6%)
  local copies, waits for them, and re-layouts  5.52 us (4%)
    all_to_all x1, waiting for transfers between devices, shards(): lax.all_to_all(spectra, 'shard', split_axis=0, concat_axis=0, tiled=True)  42.2 us
    pallas_call x1, Pallas kernels, phase_tables(): pl.pallas_call(phase_body, out_shape=jax.ShapeDtypeStruct((MODF, 2, CHANS...  13.8 us
    all_to_all x1, starting transfers between devices, shards(): lax.all_to_all(spectra, 'shard', split_axis=0, concat_axis=0, tiled=True)  13.3 us
    pallas_call x1, Pallas kernels, channelize(): pl.pallas_call(channelize_body, out_shape=jax.ShapeDtypeStruct((2 * CHANS...  10.7 us
    pallas_call x1, Pallas kernels, calibrate(): pl.pallas_call(calibrate_body, out_shape=(jax.ShapeDtypeStruct((2, rows,...  10 us
    pallas_call x1, Pallas kernels, dedisperse(): pl.pallas_call(dedisperse_body, out_shape=jax.ShapeDtypeStruct((MODF, 2 *...  9.37 us
    pallas_call x1, Pallas kernels, form_beams(): pl.pallas_call(beam_body, out_shape=jax.ShapeDtypeStruct((SHARDS, LOCAL,...  9.13 us
    all_to_all x1, starting transfers between devices, shards(): lax.all_to_all(modulated, 'shard', split_axis=0, concat_axis=0, tiled=True)  8.98 us
  transfers between devices with their start and end apart: 2, of which 2 were waited for; matrix products, arithmetic and copies ran while one was open for 1% of the time, Pallas kernels for 13%

profile of v1, /device:TPU:1, one launch (start us, length us, event | category | flops | bytes accessed | tf_op | source)
XLA Modules:
  0.0 141.4 jit_solution(16878729127541491214)
XLA Ops:
  0.0 10.7 %channelize.1 = bf16[2048,512]{1,0:T(8,128)(2,1)} custom-call(bf16[2048,2048]{1,0:T(8,128)(2,1)} %constant.27.table_ref, bf16[2,16,32768]{2,1,0:T(8,128)(2,1)} %bitcast.11), custom_call_target="tpu_custom_call" | custom-call | tf_op jit(solution)/shard_map/channelize/pallas_call | solution.py:70
  10.7 0.0 copy-start.2
  10.8 0.0 copy-start.4
  10.8 13.3 %all-to-all-start = ((bf16[64,32,512]{2,1,0:T(8,128)(2,1)}), bf16[64,32,512]{2,1,0:T(8,128)(2,1)S(1)}, u32[]{:S(2)}, u32[]{:S(2)}) async-start(bf16[64,32,512]{2,1,0:T(8,128)(2,1)} %bitcast.10), calls=%async_computation | async-start | bytes 4194304 | tf_op jit(solution)/shard_map/all_to_all | solution.py:321
  24.1 0.0 copy-done.2
  24.1 1.0 copy.8.cell_ref
  25.1 0.0 copy-done.4
  25.1 0.6 dynamic-slice
  26.4 5.2 %beam_table.1.table_ref = bf16[2,1024,1024]{2,1,0:T(8,128)(2,1)} custom-call(s32[1024,1]{1,0:T(8,128)} %copy.8.cell_ref, bf16[256,512]{1,0:T(8,128)(2,1)} %constant.28.rows_ref), custom_call_target="tpu_custom_call" | custom-call | tf_op jit(solution)/shard_map/beam_table/pallas_call | solution.py:139
  31.5 0.0 copy-start.3
  31.6 42.2 %all-to-all-done.data_ref = bf16[64,32,512]{2,1,0:T(8,128)(2,1)S(1)} async-done(((bf16[64,32,512]{2,1,0:T(8,128)(2,1)}), bf16[64,32,512]{2,1,0:T(8,128)(2,1)S(1)}, u32[]{:S(2)}, u32[]{:S(2)}) %all-to-all-start) | async-done | bytes 2097184 | tf_op jit(solution)/shard_map/all_to_all | solution.py:321
  73.8 0.0 copy-start
  73.8 1.3 copy-done
  75.1 10.0 %calibrate.1 = (bf16[2,512,1024]{2,1,0:T(8,128)(2,1)}, f32[16,128]{1,0:T(8,128)}) custom-call(bf16[64,32,512]{2,1,0:T(8,128)(2,1)} %copy-done, bf16[2,16,1024]{2,1,0:T(8,128)(2,1)} %gain_ref.1), custom_call_target="tpu_custom_call" | custom-call | tf_op jit(solution)/shard_map/calibrate/pallas_call | solution.py:203
  85.1 0.8 slice_reduce_fusion
  86.0 0.2 dynamic-update-slice
  86.2 8.4 %all-reduce = f32[64]{0:T(128)S(1)} all-reduce(f32[64]{0:T(128)S(1)} %dynamic-update-slice), channel_id=2, replica_groups=mesh['section'=4,'shard'=64] {'section'}, use_global_device_ids=true, to_apply=%add | all-reduce | flops 64 | bytes 512
  94.6 0.0 copy-done.3
  94.6 0.1 fusion
  94.7 0.7 broadcast_in_dim.4.scale_ref
  95.4 9.1 %beams.1 = bf16[64,16,256]{2,1,0:T(8,128)(2,1)} custom-call(bf16[2,512,1024]{2,1,0:T(8,128)(2,1)} %get-tuple-element.7.cal_ref, bf16[2,1024,1024]{2,1,0:T(8,128)(2,1)} %beam_table.1.table_ref, f32[16,128]{1,0:T(8,128)} %broadcast_in_dim.4.scale_ref), custom_call_target="tpu_custom_call" | custom-call | tf_op jit(solution)/shard_map/beams/pallas_call | solution.py:271
  104.5 9.0 %all-to-all-start.1 = ((bf16[64,16,256]{2,1,0:T(8,128)(2,1)}), bf16[64,16,256]{2,1,0:T(8,128)(2,1)S(1)}, u32[]{:S(2)}, u32[]{:S(2)}) async-start(bf16[64,16,256]{2,1,0:T(8,128)(2,1)} %beams.1), calls=%async_computation.1 | async-start | bytes 1048576 | tf_op jit(solution)/shard_map/all_to_all | solution.py:335
  113.5 13.8 %phases.1.phase_ref = bf16[7,2,1024,512]{3,2,1,0:T(8,128)(2,1)} custom-call(s32[1024,512]{1,0:T(8,128)} %delay_ref.1), custom_call_target="tpu_custom_call" | custom-call | tf_op jit(solution)/shard_map/phases/pallas_call | solution.py:109
  127.3 3.9 %all-to-all-done.1 = bf16[64,16,256]{2,1,0:T(8,128)(2,1)S(1)} async-done(((bf16[64,16,256]{2,1,0:T(8,128)(2,1)}), bf16[64,16,256]{2,1,0:T(8,128)(2,1)S(1)}, u32[]{:S(2)}, u32[]{:S(2)}) %all-to-all-start.1) | async-done | bytes 524320 | tf_op jit(solution)/shard_map/all_to_all | solution.py:335
  131.2 0.0 copy-start.1
  131.2 0.8 copy-done.1
  132.0 9.4 %dedisperse.1 = bf16[7,32,512]{2,1,0:T(8,128)(2,1)} custom-call(bf16[1024,256]{1,0:T(8,128)(2,1)} %bitcast.12, bf16[7,2,1024,512]{3,2,1,0:T(8,128)(2,1)} %phases.1.phase_ref), custom_call_target="tpu_custom_call" | custom-call | tf_op jit(solution)/shard_map/dedisperse/pallas_call | solution.py:304
  (1 shorter events, 0.0 us)
Async XLA Ops:
  10.7 13.3 %copy-start.2 = (s32[1024]{0:T(1024)S(1)}, s32[1024]{0:T(1024)}, u32[]{:S(2)}) copy-start(s32[1024]{0:T(1024)} %param.9) | copy-start | bytes 12292
  10.8 14.4 %copy-start.4 = (u32[256]{0:T(256)S(1)}, u32[256]{0:T(256)}, u32[]{:S(2)}) copy-start(u32[256]{0:T(256)} %constant.31) | copy-start | bytes 3076
  10.8 63.0 %all-to-all-start = ((bf16[64,32,512]{2,1,0:T(8,128)(2,1)}), bf16[64,32,512]{2,1,0:T(8,128)(2,1)S(1)}, u32[]{:S(2)}, u32[]{:S(2)}) async-start(bf16[64,32,512]{2,1,0:T(8,128)(2,1)} %bitcast.10), calls=%async_computation | async-start | bytes 4194304 | tf_op jit(solution)/shard_map/all_to_all | solution.py:321
  31.5 63.1 %copy-start.3 = (f32[16]{0:T(128)S(1)}, f32[16]{0:T(128)}, u32[]{:S(2)}) copy-start(f32[16]{0:T(128)} %param.10) | copy-start | bytes 196
  73.8 1.3 copy-start
  104.5 26.7 %all-to-all-start.1 = ((bf16[64,16,256]{2,1,0:T(8,128)(2,1)}), bf16[64,16,256]{2,1,0:T(8,128)(2,1)S(1)}, u32[]{:S(2)}, u32[]{:S(2)}) async-start(bf16[64,16,256]{2,1,0:T(8,128)(2,1)} %beams.1), calls=%async_computation.1 | async-start | bytes 1048576 | tf_op jit(solution)/shard_map/all_to_all | solution.py:335
  131.2 0.8 copy-start.1

commit v2 on v0

v2 whole, which is shorter than its diff:
```python
import math

import jax
import jax.numpy as jnp
import numpy as np
from jax import lax
from jax.experimental import pallas as pl
from jax.experimental.pallas import tpu as pltpu
from jax.sharding import PartitionSpec as P

POL = 2
GRID_X = 4
GRID_Y = 256
NSAMP = 2048
TDFT = 16
TRIALS = 512
FEEDS = 1024
CHANS = 1024
MODF = 7
BLOCKS = 4
SHARDS = 64
LOCAL = 16
HALF = LOCAL // 2
ROWS = POL * TDFT * LOCAL
FOLD = NSAMP // 2
VMEM_LIMIT = 62 * 1024 * 1024
MESH = pl.DeviceIdType.MESH


def spectral_constant():
    shape = (2, SHARDS, 2, HALF)
    parity, dest, part, chan = np.meshgrid(*[np.arange(n) for n in shape], indexing="ij")
    chans = (dest * LOCAL + 2 * chan + parity)[..., None].astype(np.int64)
    cols = np.arange(FOLD, dtype=np.int64)
    angles = np.float32(2.0 * math.pi / NSAMP) * (chans * cols % NSAMP).astype(np.float32)
    table = np.where(part[..., None] == 0, np.cos(angles), -np.sin(angles)).astype(np.float32)
    return jnp.asarray(table.reshape(2, CHANS, FOLD)).astype(jnp.bfloat16)


def row_constant():
    rows = np.arange(GRID_Y)[:, None]
    cols = np.arange(GRID_Y)[None, :]
    angles = np.float32(2.0 * math.pi / GRID_Y) * (rows * cols % GRID_Y).astype(np.float32)
    table = np.concatenate([np.cos(angles), np.sin(angles)], 1).astype(np.float32)
    return jnp.asarray(table).astype(jnp.bfloat16)


def frame_matrix():
    frames = np.arange(TDFT)[:, None]
    freqs = np.arange(1, MODF + 1)[None, :]
    angles = 2.0 * math.pi / TDFT * (frames * freqs % TDFT)
    return np.concatenate([np.cos(angles), -np.sin(angles)], 1) / math.sqrt(TDFT)


def cosine_of(step):
    fold = jnp.abs(8 - step)
    out = jnp.full(step.shape, -math.cos(0.0), jnp.float32)
    for entry in range(1, 9):
        out = jnp.where(fold == entry, np.float32(-math.cos(2.0 * math.pi * entry / TDFT)), out)
    return out


def exchange(parts):
    parts = list(parts)
    lane = lax.broadcasted_iota(jnp.int32, parts[0].shape, 1)
    for bit in (4, 2, 1):
        upper = (lane & (bit * LOCAL)) != 0
        for i in range(8):
            if i & bit:
                continue
            low, high = parts[i], parts[i + bit]
            parts[i] = jnp.where(upper, pltpu.roll(high, bit * LOCAL, 1), low)
            parts[i + bit] = jnp.where(upper, high, pltpu.roll(low, 128 - bit * LOCAL, 1))
    return parts


def frame_transform(power):
    half = TDFT // 2
    table = frame_matrix()
    plus = [power[n] + power[n + half] for n in range(half)]
    minus = [power[n] - power[n + half] for n in range(half)]
    out = []
    for q in range(2 * MODF):
        source = minus if (q % MODF + 1) % 2 else plus
        total = None
        for n in range(half):
            factor = float(table[n, q])
            if abs(factor) < 1e-12:
                continue
            term = source[n] * np.float32(factor)
            total = term if total is None else total + term
        out.append(total)
    return out


def dot(a, b):
    return jnp.dot(a, b, preferred_element_type=jnp.float32)


def column(row):
    shape = (128, 128)
    same = lax.broadcasted_iota(jnp.int32, shape, 0) == lax.broadcasted_iota(jnp.int32, shape, 1)
    return jnp.sum(jnp.where(same, jnp.broadcast_to(row, shape), 0.0), axis=1, keepdims=True)


def body(
    volts_hbm, table_hbm, gain_hbm, delay_hbm, cell_ref, decay_ref, row_ref, out_ref,
    volts, table, gain_in, delay, folded, send, recv, gain, cal, beam_tab, phase, power,
    send_two, recv_two, turned, total_ref, level_send, level_recv,
    load_sem, own_sem, send_sem, recv_sem, send_two_sem, recv_two_sem, level_send_sem, level_recv_sem,
):
    me = lax.axis_index("shard")
    place = lax.axis_index("section")
    my_z, low = me // 8, me % 8

    loads = [
        pltpu.make_async_copy(volts_hbm.at[0], volts.at[0], load_sem.at[0]),
        pltpu.make_async_copy(table_hbm.at[0], table.at[0], load_sem.at[1]),
        pltpu.make_async_copy(volts_hbm.at[1], volts.at[1], load_sem.at[2]),
        pltpu.make_async_copy(table_hbm.at[1], table.at[1], load_sem.at[3]),
        pltpu.make_async_copy(gain_hbm, gain_in, load_sem.at[4]),
    ] + [
        pltpu.make_async_copy(
            delay_hbm.at[:, pl.ds(tile * 128, 128)], delay.at[tile], load_sem.at[5 + tile]
        )
        for tile in range(4)
    ]
    for load in loads:
        load.start()

    barrier = pltpu.get_barrier_semaphore()

    def greet(i, carry):
        pl.semaphore_signal(barrier, inc=1, device_id={"shard": (me + i) % SHARDS}, device_id_type=MESH)
        return carry

    lax.fori_loop(1, SHARDS, greet, 0)
    for i in range(1, BLOCKS):
        pl.semaphore_signal(
            barrier, inc=1, device_id={"section": (place + i) % BLOCKS}, device_id_type=MESH
        )

    for pol in range(POL):
        loads[2 * pol].wait()

        def fold(frame, carry):
            first = pl.ds(pl.multiple_of(frame * NSAMP, NSAMP), FOLD)
            second = pl.ds(pl.multiple_of(frame * NSAMP + FOLD, FOLD), FOLD)
            a = volts[pol, :, first].astype(jnp.float32)
            b = volts[pol, :, second].astype(jnp.float32)
            rows = pl.ds(pl.multiple_of((pol * TDFT + frame) * LOCAL, LOCAL), LOCAL)
            folded[0, rows, :] = (a + b).astype(jnp.bfloat16)
            folded[1, rows, :] = (a - b).astype(jnp.bfloat16)
            return carry

        lax.fori_loop(0, TDFT, fold, 0)

    def plane_of(i):
        step, odd = i // 2, i % 2
        return (my_z + 4 + step - odd * (2 * step + 1) + 8) % 8

    def send_one(half, dest):
        pltpu.make_async_remote_copy(
            send.at[half, dest], recv.at[half, me], send_sem.at[half], recv_sem.at[half, my_z],
            device_id={"shard": dest}, device_id_type=MESH,
        ).start()

    def send_plane(half, i):
        z = plane_of(i)

        def one(r, carry):
            send_one(half, z * 8 + (low + r) % 8)
            return carry

        lax.fori_loop(0, 8, one, 0)

    own = [
        pltpu.make_async_copy(send.at[half, me], recv.at[half, me], own_sem.at[half])
        for half in range(2)
    ]

    for half in range(2):
        loads[1 + 2 * half].wait()

        def channelize(i, carry):
            z = plane_of(i)
            rows = pl.ds(pl.multiple_of(z * 128, 128), 128)
            spectra = lax.dot_general(
                table[half, rows, :], folded[half], (((1,), (1,)), ((), ())),
                preferred_element_type=jnp.float32,
            )
            spectra = (spectra * (1.0 / math.sqrt(NSAMP))).astype(jnp.bfloat16)
            send[half, pl.ds(pl.multiple_of(z * 8, 8), 8)] = spectra.reshape(8, LOCAL, ROWS)

            @pl.when(i > 0)
            def _():
                if half == 0:

                    @pl.when(i == 1)
                    def _():
                        pl.semaphore_wait(barrier, SHARDS - 1 + BLOCKS - 1)

                send_plane(half, i - 1)

            return carry

        lax.fori_loop(0, 8, channelize, 0)

        def last(r, carry):
            send_one(half, my_z * 8 + (low + r) % 8)
            return carry

        lax.fori_loop(1, 8, last, 0)
        own[half].start()

    loads[4].wait()
    for half in range(2):
        shape = (HALF, LOCAL)
        pick = lax.broadcasted_iota(jnp.int32, shape, 1) == (
            2 * lax.broadcasted_iota(jnp.int32, shape, 0) + half
        )
        pick = pick.astype(jnp.float32).astype(jnp.bfloat16)
        for part in range(2):
            gain[half, part] = dot(pick, gain_in[part])

    def beam_rows(i, carry):
        cell = cell_ref[pl.ds(i, 1), :]
        x, y = cell // GRID_Y, cell % GRID_Y
        rows = pl.ds(pl.multiple_of(i * 128, 128), 128)
        y_column = column(y.astype(jnp.float32))
        lanes = lax.broadcasted_iota(jnp.int32, (128, GRID_Y), 1).astype(jnp.float32)
        hot = (lanes == y_column).astype(jnp.float32).astype(jnp.bfloat16)
        both = dot(hot, row_ref[...])
        cos, sin = both[:, :GRID_Y], both[:, GRID_Y:]
        for u in range(GRID_X):
            turn = column(((u * x) % 4).astype(jnp.float32))
            real = jnp.where(turn == 0, cos, jnp.where(turn == 1, -sin, jnp.where(turn == 2, -cos, sin)))
            imag = jnp.where(turn == 0, -sin, jnp.where(turn == 1, -cos, jnp.where(turn == 2, sin, cos)))
            beam_tab[0, rows, u * GRID_Y : (u + 1) * GRID_Y] = real.astype(jnp.bfloat16)
            beam_tab[1, rows, u * GRID_Y : (u + 1) * GRID_Y] = imag.astype(jnp.bfloat16)
        return carry

    lax.fori_loop(0, 8, beam_rows, 0)

    for load in loads[5:]:
        load.wait()
    for half in range(2):

        def phases(i, carry):
            tile, block = i // 8, i % 8
            step = delay[tile, pl.ds(half + 128 * block, 64, stride=2), :] & (TDFT - 1)
            rows = pl.ds(pl.multiple_of(half * 512 + block * 64, 64), 64)
            lanes = pl.ds(pl.multiple_of(tile * 128, 128), 128)
            sign = (1 - 2 * (step & 1)).astype(jnp.float32)
            cos, sin = cosine_of(step), cosine_of((step + 12) & (TDFT - 1))
            twice = 2.0 * cos
            cos_now, sin_now = cos, sin
            cos_last, sin_last = jnp.ones_like(cos), jnp.zeros_like(cos)
            for f in range(1, 5):
                phase[f - 1, 0, rows, lanes] = cos_now.astype(jnp.bfloat16)
                phase[f - 1, 1, rows, lanes] = sin_now.astype(jnp.bfloat16)
                if f < 4:
                    phase[7 - f, 0, rows, lanes] = (sign * cos_now).astype(jnp.bfloat16)
                    phase[7 - f, 1, rows, lanes] = (-sign * sin_now).astype(jnp.bfloat16)
                    cos_now, cos_last = twice * cos_now - cos_last, cos_now
                    sin_now, sin_last = twice * sin_now - sin_last, sin_now
            return carry

        lax.fori_loop(0, 32, phases, 0)

    offset = frame_matrix().sum(0)

    def calibrate(half, octet):
        feeds = pl.ds(pl.multiple_of(octet * 128, 128), 128)
        gain_real, gain_imag = gain[half, 0, :, feeds], gain[half, 1, :, feeds]

        def one(tile, total):
            lanes = pl.ds(pl.multiple_of(tile * 128, 128), 128)
            parts = [recv[half, octet * 8 + s, :, lanes].astype(jnp.float32) for s in range(8)]
            parts = exchange(parts)
            for n in range(0, 8, 2):
                reals, imags = [], []
                for part in parts[n : n + 2]:
                    real, imag = part[:HALF], part[HALF:]
                    reals.append(gain_real * real - gain_imag * imag)
                    imags.append(gain_real * imag + gain_imag * real)
                rows = pl.ds(pl.multiple_of(tile * 64 + n * HALF, LOCAL), LOCAL)
                for which, values in enumerate((reals, imags)):
                    value = jnp.concatenate(values, 0).astype(jnp.bfloat16)
                    cal[which, rows, feeds] = value
                    wide = value.astype(jnp.float32)
                    total = total + wide * wide
            return total

        return lax.fori_loop(0, 4, one, jnp.zeros((LOCAL, 128), jnp.float32))

    def arrive(half, octet, count):
        pltpu.make_async_remote_copy(
            recv.at[half, pl.ds(0, count)], recv.at[half, pl.ds(0, count)],
            send_sem.at[half], recv_sem.at[half, octet],
            device_id={"shard": me}, device_id_type=MESH,
        ).wait_recv()

    def level_copy(half, i):
        return pltpu.make_async_remote_copy(
            level_send.at[half], level_recv.at[half, place], level_send_sem.at[half, i - 1],
            level_recv_sem.at[half, place],
            device_id={"section": (place + i) % BLOCKS}, device_id_type=MESH,
        )

    def two_copy(half, dest):
        return pltpu.make_async_remote_copy(
            send_two.at[half, dest], recv_two.at[half, me], send_two_sem.at[half], recv_two_sem.at[half],
            device_id={"shard": dest}, device_id_type=MESH,
        )

    own_two = [
        pltpu.make_async_copy(send_two.at[half, me], recv_two.at[half, me], own_sem.at[2 + half])
        for half in range(2)
    ]

    for half in range(2):

        def octets(i, total):
            octet = plane_of(i)
            arrive(half, octet, 8)
            return total + calibrate(half, octet)

        total = lax.fori_loop(0, 7, octets, jnp.zeros((LOCAL, 128), jnp.float32))
        arrive(half, my_z, 7)
        own[half].wait()
        total = total + calibrate(half, my_z)
        total = jnp.sum(total[:HALF] + total[HALF:], axis=1, keepdims=True) * (1.0 / TDFT) + 1e-06
        level_send[half] = jnp.broadcast_to(total, (HALF, 128))
        level_recv[half, place] = jnp.broadcast_to(total, (HALF, 128))

        decay_row = jnp.broadcast_to(decay_ref[...], (HALF, LOCAL))
        pick = lax.broadcasted_iota(jnp.int32, (HALF, LOCAL), 1) == (
            2 * lax.broadcasted_iota(jnp.int32, (HALF, LOCAL), 0) + half
        )
        decay = jnp.sum(jnp.where(pick, decay_row, 0.0), axis=1, keepdims=True)
        decay = jnp.broadcast_to(decay, (HALF, 128))

        def beams(i, carry):
            wide = pl.ds(pl.multiple_of(i * 256, 256), 256)
            real_tab, imag_tab = beam_tab[0, :, wide], beam_tab[1, :, wide]
            real = dot(cal[0], real_tab) - dot(cal[1], imag_tab)
            imag = dot(cal[0], imag_tab) + dot(cal[1], real_tab)
            both = real * real + imag * imag
            power[i] = both[:128] + both[128:]

            return carry

        for i in range(1, BLOCKS):
            level_copy(half, i).start()
        lax.fori_loop(0, 4, beams, 0)
        for i in range(1, BLOCKS):
            other = (place + i) % BLOCKS
            pltpu.make_async_remote_copy(
                level_send.at[half], level_recv.at[half, other], level_send_sem.at[half, i - 1],
                level_recv_sem.at[half, other],
                device_id={"section": other}, device_id_type=MESH,
            ).wait_recv()
        dividend = jnp.zeros((HALF, 128), jnp.float32)
        divisor = jnp.zeros((HALF, 128), jnp.float32)
        for block in range(BLOCKS):
            use = block <= place
            dividend = jnp.where(use, decay * dividend + level_recv[half, block], dividend)
            divisor = jnp.where(use, decay * divisor + 1.0, divisor)
        scale = divisor / dividend

        def modulate(i, carry):
            for tile in range(2):
                lanes = slice(tile * 128, (tile + 1) * 128)
                frames = [power[i, n * HALF : (n + 1) * HALF, lanes] for n in range(TDFT)]
                freqs = frame_transform(frames)
                freqs = [v * scale - np.float32(offset[q]) for q, v in enumerate(freqs)]
                freqs = freqs + [jnp.zeros_like(scale)] * 2
                first, second = exchange(freqs[:8]), exchange(freqs[8:])
                for j in range(8):
                    both = jnp.concatenate([first[j], second[j]], 0)
                    send_two[half, i * 16 + tile * 8 + j] = both.astype(jnp.bfloat16)
            return carry

        lax.fori_loop(0, 4, modulate, 0)

        def send_rest(i, carry):
            two_copy(half, (me + i) % SHARDS).start()
            return carry

        lax.fori_loop(1, SHARDS, send_rest, 0)
        own_two[half].start()

    for half in range(2):
        pltpu.make_async_remote_copy(
            recv_two.at[half, pl.ds(0, SHARDS - 1)], recv_two.at[half, pl.ds(0, SHARDS - 1)],
            send_two_sem.at[half], recv_two_sem.at[half],
            device_id={"shard": me}, device_id_type=MESH,
        ).wait_recv()
        own_two[half].wait()
        data = recv_two[half].astype(jnp.float32)
        for group in range(2):
            rows = data[:, group * HALF : (group + 1) * HALF, :].reshape(SHARDS * HALF, 128)
            turned[group * 128 : (group + 1) * 128, :] = rows.T.astype(jnp.bfloat16)

        def dedisperse(f, carry):
            real = turned[pl.ds(pl.multiple_of(f * LOCAL, LOCAL), LOCAL), :]
            imag = turned[pl.ds(pl.multiple_of((f + MODF) * LOCAL, LOCAL), LOCAL), :]
            rows = slice(half * 512, (half + 1) * 512)
            total = dot(jnp.concatenate([real, imag], 0), phase[f, 0, rows, :])
            total = total + dot(jnp.concatenate([imag, -real], 0), phase[f, 1, rows, :])
            if half == 0:
                total_ref[f] = total
            else:
                total = total + total_ref[f]
                out_ref[f] = (total * (1.0 / math.sqrt(CHANS))).astype(jnp.bfloat16)
            return carry

        lax.fori_loop(0, MODF, dedisperse, 0)

    for half in range(2):
        pltpu.make_async_remote_copy(
            send.at[half, pl.ds(0, SHARDS - 1)], recv.at[half, pl.ds(0, SHARDS - 1)],
            send_sem.at[half], recv_sem.at[half, 0],
            device_id={"shard": me}, device_id_type=MESH,
        ).wait_send()
        pltpu.make_async_remote_copy(
            send_two.at[half, pl.ds(0, SHARDS - 1)], recv_two.at[half, pl.ds(0, SHARDS - 1)],
            send_two_sem.at[half], recv_two_sem.at[half],
            device_id={"shard": me}, device_id_type=MESH,
        ).wait_send()
        for i in range(1, BLOCKS):
            level_copy(half, i).wait_send()


def shards(voltages, feed_gains, grid_index, decay_rates, delays):
    bf16, f32 = jnp.bfloat16, jnp.float32
    anywhere = pl.BlockSpec(memory_space=pl.ANY)
    here = pl.BlockSpec(memory_space=pltpu.VMEM)
    dma = pltpu.SemaphoreType.DMA
    out = pl.pallas_call(
        body,
        out_shape=jax.ShapeDtypeStruct((MODF, 2 * LOCAL, TRIALS), bf16),
        in_specs=[anywhere] * 4 + [here] * 3,
        out_specs=here,
        scratch_shapes=[
            pltpu.VMEM((POL, LOCAL, TDFT * NSAMP), bf16),
            pltpu.VMEM((2, CHANS, FOLD), bf16),
            pltpu.VMEM((2, LOCAL, FEEDS), bf16),
            pltpu.VMEM((4, CHANS, 128), jnp.int32),
            pltpu.VMEM((2, ROWS, FOLD), bf16),
            pltpu.VMEM((2, SHARDS, LOCAL, ROWS), bf16),
            pltpu.VMEM((2, SHARDS, LOCAL, ROWS), bf16),
            pltpu.VMEM((2, 2, HALF, FEEDS), f32),
            pltpu.VMEM((2, ROWS // 2, FEEDS), bf16),
            pltpu.VMEM((2, FEEDS, FEEDS), bf16),
            pltpu.VMEM((MODF, 2, CHANS, TRIALS), bf16),
            pltpu.VMEM((4, TDFT * HALF, 256), f32),
            pltpu.VMEM((2, SHARDS, LOCAL, 128), bf16),
            pltpu.VMEM((2, SHARDS, LOCAL, 128), bf16),
            pltpu.VMEM((256, SHARDS * HALF), bf16),
            pltpu.VMEM((MODF, 2 * LOCAL, TRIALS), f32),
            pltpu.VMEM((2, HALF, 128), f32),
            pltpu.VMEM((2, BLOCKS, HALF, 128), f32),
            dma((9,)), dma((4,)), dma((2,)), dma((2, 8)), dma((2,)), dma((2,)),
            dma((2, BLOCKS - 1)), dma((2, BLOCKS)),
        ],
        compiler_params=pltpu.CompilerParams(
            collective_id=0, has_side_effects=True, vmem_limit_bytes=VMEM_LIMIT
        ),
        name="telescope",
    )(
        voltages[0], spectral_constant(), feed_gains, delays,
        grid_index.reshape(8, 128), decay_rates.reshape(1, LOCAL), row_constant(),
    )
    return out.reshape(MODF, 2, LOCAL, TRIALS).transpose(0, 3, 1, 2)[None]


def solution(mesh):
    in_specs = (P("section", None, "shard", None), P(None, "shard", None), P(), P("shard"), P())
    out_specs = P("section", None, None, None, "shard")
    return jax.shard_map(shards, mesh=mesh, in_specs=in_specs, out_specs=out_specs, check_vma=False)
```

time: 516 us -> 83.4 us (0.16); the launches traced: 510 us -> 83.3 us
  matrix products: 217 us -> 0 us
  local copies, waits for them, and re-layouts: 131 us -> 1.64 us
  Pallas kernels: 0 us -> 81.6 us
  waiting for transfers between devices: 55.8 us -> 0 us
  other arithmetic: 47.6 us -> 0 us
  loops' own time: 27.1 us -> 0 us
  starting transfers between devices: 22.3 us -> 0 us
  blocking collectives: 8.44 us -> 0 us
    dot_general x32 -> x0, matrix products: 217 us -> none  [the longest x7 48.5 us: per_frequency(): lax.dot_general(sine_part, mod_imag, contract, preferred_element_type=jnp...]
    pallas_call x0 -> x1, Pallas kernels: none -> 81.6 us  [shards(): pl.pallas_call(body, out_shape=jax.ShapeDtypeStruct((MODF, 2 * LOCAL, TRI...]
    all_to_all x2 -> x0, waiting for transfers between devices: 55.8 us -> none  [the longest x1 40.2 us: shards(): lax.all_to_all(spectra, 'shard', split_axis=1, concat_axis=3, tiled=True)]
    gather x2 -> x0, local copies, waits for them, and re-layouts: 37.3 us -> none  [form_beams(): jnp.take(calibrated, cell_feed, axis=3)]
    another operation x2 -> x0, loops' own time: 27.1 us -> none  [the longest x1 27.1 us: dedisperse(): return lax.map(per_frequency, jnp.arange(MODF, dtype=jnp.int32))]
    slice x5 -> x0, local copies, waits for them, and re-layouts: 23.2 us -> none  [form_beams(): real_part = gain_values[0] * values[0] - gain_values[1] * values[1]]
    all_to_all x2 -> x0, starting transfers between devices: 22.3 us -> none  [the longest x1 13.3 us: shards(): lax.all_to_all(spectra, 'shard', split_axis=1, concat_axis=3, tiled=True)]
    another operation x6 -> x0, local copies, waits for them, and re-layouts: 19.2 us -> none  [the longest x1 16.1 us: form_beams(): calibrated = jnp.stack([real_part, imag_part]).astype(jnp.bfloat16)]
  transfers between devices with their start and end apart: 2 -> 0, of which waited for: 2 -> 0; matrix products, arithmetic and copies ran while one was open for 2% -> 0% of each run, Pallas kernels for 0% -> 0%
where the time goes in v2:
time: 83.4 us; the launch traced here: 83.3 us
  Pallas kernels  81.6 us (98%)
  local copies, waits for them, and re-layouts  1.64 us (2%)
    pallas_call x1, Pallas kernels, shards(): pl.pallas_call(body, out_shape=jax.ShapeDtypeStruct((MODF, 2 * LOCAL, TRI...  81.6 us

profile of v2, /device:TPU:1, one launch (start us, length us, event | category | flops | bytes accessed | tf_op | source)
XLA Modules:
  0.0 83.3 jit_solution(8488716471102334675)
XLA Ops:
  0.0 81.6 %telescope.1 = bf16[7,32,512]{2,1,0:T(8,128)(2,1)} custom-call(bf16[2,16,32768]{2,1,0:T(8,128)(2,1)} %bitcast.8, bf16[2,1024,1024]{2,1,0:T(8,128)(2,1)} %constant.9.table_hbm, bf16[2,16,1024]{2,1,0:T(8,128)(2,1)} %gain_hbm.1, s32[1024,512]{1,0:T(8,128)} %delay_hbm.1, s32[8,128]{1,0:T(8,128)} %bitcast.10, f32[1,16]{1,0:T(1,128)} %bitcast.11, ...), custom_call_target="tpu_custom_call" | custom-call | tf_op jit(solution)/shard_map/telescope/pallas_call | solution.py:441
  81.7 1.6 %copy.9 = bf16[1,7,512,2,16]{2,4,3,1,0:T(8,128)(2,1)} copy(bf16[1,7,512,2,16]{2,4,3,1,0:T(8,128)(2,1)} %bitcast.9) | data formatting | bytes 458752

commit v3 on v2

v3 whole, which is shorter than its diff:
```python
import math

import jax
import jax.numpy as jnp
import numpy as np
from jax import lax
from jax.experimental import pallas as pl
from jax.experimental.pallas import tpu as pltpu
from jax.sharding import PartitionSpec as P

POL = 2
GRID_X = 4
GRID_Y = 256
NSAMP = 2048
TDFT = 16
TRIALS = 512
FEEDS = 1024
CHANS = 1024
MODF = 7
BLOCKS = 4
SHARDS = 64
LOCAL = 16
QUARTER = LOCAL // 4
PIECES = 4
CLASSES = (0, 2, 1, 3)
ROWS = POL * TDFT * LOCAL
PIECE = SHARDS * 2 * QUARTER
VMEM_LIMIT = 62 * 1024 * 1024
MESH = pl.DeviceIdType.MESH


def spectral_constant(classes, length):
    shape = (len(classes), SHARDS, 2, QUARTER)
    which, dest, part, chan = np.meshgrid(*[np.arange(n) for n in shape], indexing="ij")
    chans = (dest * LOCAL + 4 * chan + np.asarray(classes)[which])[..., None].astype(np.int64)
    cols = np.arange(length, dtype=np.int64)
    angles = np.float32(2.0 * math.pi / NSAMP) * (chans * cols % NSAMP).astype(np.float32)
    table = np.where(part[..., None] == 0, np.cos(angles), -np.sin(angles)).astype(np.float32)
    return jnp.asarray(table.reshape(len(classes), PIECE, length)).astype(jnp.bfloat16)


def row_constant():
    rows = np.arange(GRID_Y)[:, None]
    cols = np.arange(GRID_Y)[None, :]
    angles = np.float32(2.0 * math.pi / GRID_Y) * (rows * cols % GRID_Y).astype(np.float32)
    table = np.concatenate([np.cos(angles), np.sin(angles)], 1).astype(np.float32)
    return jnp.asarray(table).astype(jnp.bfloat16)


def frame_matrix():
    frames = np.arange(TDFT)[:, None]
    freqs = np.arange(1, MODF + 1)[None, :]
    angles = 2.0 * math.pi / TDFT * (frames * freqs % TDFT)
    return np.concatenate([np.cos(angles), -np.sin(angles)], 1) / math.sqrt(TDFT)


def cosine_of(step):
    fold = jnp.abs(8 - step)
    out = jnp.full(step.shape, -math.cos(0.0), jnp.float32)
    for entry in range(1, 9):
        out = jnp.where(fold == entry, np.float32(-math.cos(2.0 * math.pi * entry / TDFT)), out)
    return out


def exchange(parts):
    parts = list(parts)
    lane = lax.broadcasted_iota(jnp.int32, parts[0].shape, 1)
    for bit in (4, 2, 1):
        upper = (lane & (bit * LOCAL)) != 0
        for i in range(8):
            if i & bit:
                continue
            low, high = parts[i], parts[i + bit]
            parts[i] = jnp.where(upper, pltpu.roll(high, bit * LOCAL, 1), low)
            parts[i + bit] = jnp.where(upper, high, pltpu.roll(low, 128 - bit * LOCAL, 1))
    return parts


def dot(a, b):
    return jnp.dot(a, b, preferred_element_type=jnp.float32)


def column(row):
    shape = (128, 128)
    same = lax.broadcasted_iota(jnp.int32, shape, 0) == lax.broadcasted_iota(jnp.int32, shape, 1)
    return jnp.sum(jnp.where(same, jnp.broadcast_to(row, shape), 0.0), axis=1, keepdims=True)


def body(
    volts_hbm, even_hbm, odd_hbm, gain_hbm, delay_hbm, cell_ref, decay_ref, row_ref, out_ref,
    volts, even, odd, gain_in, delay, fold_even, fold_odd, send, recv, gain, cal, beam_tab, phase, power,
    send_two, recv_two, turned, total_ref, level_send, level_recv,
    load_sem, own_sem, send_sem, recv_sem, send_two_sem, recv_two_sem, level_send_sem, level_recv_sem,
):
    f32, bf16 = jnp.float32, jnp.bfloat16
    me = lax.axis_index("shard")
    place = lax.axis_index("section")
    my_z, low = me // 8, me % 8

    load_volts = [
        pltpu.make_async_copy(volts_hbm.at[pol], volts.at[pol], load_sem.at[pol]) for pol in range(POL)
    ]
    load_even = [
        pltpu.make_async_copy(even_hbm.at[c], even.at[c], load_sem.at[2 + c]) for c in range(2)
    ]
    load_odd = [
        pltpu.make_async_copy(odd_hbm.at[c], odd.at[c], load_sem.at[4 + c]) for c in range(2)
    ]
    load_gain = pltpu.make_async_copy(gain_hbm, gain_in, load_sem.at[6])
    load_delay = [
        pltpu.make_async_copy(
            delay_hbm.at[:, pl.ds(tile * 128, 128)], delay.at[tile], load_sem.at[7 + tile]
        )
        for tile in range(4)
    ]
    for load in load_volts + load_even + load_odd + [load_gain] + load_delay:
        load.start()

    barrier = pltpu.get_barrier_semaphore()

    def greet(i, carry):
        pl.semaphore_signal(barrier, inc=1, device_id={"shard": (me + i) % SHARDS}, device_id_type=MESH)
        return carry

    lax.fori_loop(1, SHARDS, greet, 0)
    for i in range(1, BLOCKS):
        pl.semaphore_signal(
            barrier, inc=1, device_id={"section": (place + i) % BLOCKS}, device_id_type=MESH
        )

    def quarters(pol, frame):
        parts = []
        for s in range(4):
            lanes = pl.ds(pl.multiple_of(frame * NSAMP + s * 512, 512), 512)
            parts.append(volts[pol, :, lanes].astype(f32))
        return parts, pl.ds(pl.multiple_of((pol * TDFT + frame) * LOCAL, LOCAL), LOCAL)

    def fold_sum(pol):
        def one(frame, carry):
            (a, b, c, d), rows = quarters(pol, frame)
            fold_even[0, rows, :] = ((a + c) + (b + d)).astype(bf16)
            fold_even[1, rows, :] = ((a + c) - (b + d)).astype(bf16)
            return carry

        lax.fori_loop(0, TDFT, one, 0)

    def fold_difference(pol):
        def one(frame, carry):
            (a, b, c, d), rows = quarters(pol, frame)
            fold_odd[rows, :512] = (a - c).astype(bf16)
            fold_odd[rows, 512:] = (b - d).astype(bf16)
            return carry

        lax.fori_loop(0, TDFT, one, 0)

    def plane_of(i):
        step, side = i // 2, i % 2
        return (my_z + 4 + step - side * (2 * step + 1) + 8) % 8

    def send_one(piece, dest):
        pltpu.make_async_remote_copy(
            send.at[piece, dest], recv.at[piece, me], send_sem.at[piece], recv_sem.at[piece, my_z],
            device_id={"shard": dest}, device_id_type=MESH,
        ).start()

    def send_plane(piece, i):
        z = plane_of(i)

        def one(r, carry):
            send_one(piece, z * 8 + (low + r) % 8)
            return carry

        lax.fori_loop(0, 8, one, 0)

    own = [
        pltpu.make_async_copy(send.at[piece, me], recv.at[piece, me], own_sem.at[piece])
        for piece in range(PIECES)
    ]

    def channelize(piece):
        def block(i, carry):
            z = (my_z // 2 + 2 + i) % 4
            rows = pl.ds(pl.multiple_of(z * 128, 128), 128)
            table, data = (even[piece, rows, :], fold_even[piece]) if piece < 2 else (
                odd[piece - 2, rows, :], fold_odd[...]
            )
            spectra = lax.dot_general(
                table, data, (((1,), (1,)), ((), ())), preferred_element_type=f32
            )
            spectra = (spectra * (1.0 / math.sqrt(NSAMP))).reshape(16, 8, ROWS)
            both = jnp.concatenate([spectra[:, :, : ROWS // 2], spectra[:, :, ROWS // 2 :]], 1)
            send[piece, pl.ds(pl.multiple_of(z * 16, 16), 16)] = both.astype(bf16)
            return carry

        lax.fori_loop(0, 4, block, 0)

    def send_piece(piece):
        def plane(i, carry):
            send_plane(piece, i)
            return carry

        lax.fori_loop(0, 7, plane, 0)

        def last(r, carry):
            send_one(piece, my_z * 8 + (low + r) % 8)
            return carry

        lax.fori_loop(1, 8, last, 0)
        own[piece].start()

    for pol in range(POL):
        load_volts[pol].wait()
        fold_sum(pol)
    load_even[0].wait()
    channelize(0)
    pl.semaphore_wait(barrier, SHARDS - 1 + BLOCKS - 1)
    send_piece(0)
    load_even[1].wait()
    channelize(1)
    send_piece(1)
    for pol in range(POL):
        fold_difference(pol)
    for piece in (2, 3):
        load_odd[piece - 2].wait()
        channelize(piece)
        send_piece(piece)

    def chan_pick(piece):
        shape = (8, LOCAL)
        row = lax.broadcasted_iota(jnp.int32, shape, 0) % QUARTER
        return lax.broadcasted_iota(jnp.int32, shape, 1) == 4 * row + CLASSES[piece]

    lower = lax.broadcasted_iota(jnp.int32, (8, 128), 0) < QUARTER
    sign = jnp.where(lower, -1.0, 1.0).astype(f32)

    load_gain.wait()
    for piece in range(PIECES):
        pick = chan_pick(piece).astype(f32).astype(bf16)
        gain[piece, 0] = dot(pick, gain_in[0])
        gain[piece, 1] = dot(pick, gain_in[1]) * sign[:, :1]

    def beam_rows(i, carry):
        cell = cell_ref[pl.ds(i, 1), :]
        x, y = cell // GRID_Y, cell % GRID_Y
        rows = pl.ds(pl.multiple_of(i * 128, 128), 128)
        y_column = column(y.astype(f32))
        lanes = lax.broadcasted_iota(jnp.int32, (128, GRID_Y), 1).astype(f32)
        hot = (lanes == y_column).astype(f32).astype(bf16)
        both = dot(hot, row_ref[...])
        cos, sin = both[:, :GRID_Y], both[:, GRID_Y:]
        for u in range(GRID_X):
            turn = column(((u * x) % 4).astype(f32))
            real = jnp.where(turn == 0, cos, jnp.where(turn == 1, -sin, jnp.where(turn == 2, -cos, sin)))
            imag = jnp.where(turn == 0, -sin, jnp.where(turn == 1, -cos, jnp.where(turn == 2, sin, cos)))
            beam_tab[0, rows, u * GRID_Y : (u + 1) * GRID_Y] = real.astype(bf16)
            beam_tab[1, rows, u * GRID_Y : (u + 1) * GRID_Y] = imag.astype(bf16)
        return carry

    lax.fori_loop(0, 8, beam_rows, 0)

    for load in load_delay:
        load.wait()
    for piece in range(PIECES):

        def phases(i, carry):
            tile, block = i // 4, i % 4
            step = delay[tile, pl.ds(CLASSES[piece] + 256 * block, 64, stride=4), :] & (TDFT - 1)
            rows = pl.ds(pl.multiple_of(piece * 256 + block * 64, 64), 64)
            lanes = pl.ds(pl.multiple_of(tile * 128, 128), 128)
            parity = (1 - 2 * (step & 1)).astype(f32)
            cos, sin = cosine_of(step), cosine_of((step + 12) & (TDFT - 1))
            twice = 2.0 * cos
            cos_now, sin_now = cos, sin
            cos_last, sin_last = jnp.ones_like(cos), jnp.zeros_like(cos)
            for f in range(1, 5):
                phase[f - 1, 0, rows, lanes] = cos_now.astype(bf16)
                phase[f - 1, 1, rows, lanes] = sin_now.astype(bf16)
                if f < 4:
                    phase[7 - f, 0, rows, lanes] = (parity * cos_now).astype(bf16)
                    phase[7 - f, 1, rows, lanes] = (-parity * sin_now).astype(bf16)
                    cos_now, cos_last = twice * cos_now - cos_last, cos_now
                    sin_now, sin_last = twice * sin_now - sin_last, sin_now
            return carry

        lax.fori_loop(0, 16, phases, 0)

    def calibrate(piece, octet):
        feeds = pl.ds(pl.multiple_of(octet * 128, 128), 128)
        straight, crossed = gain[piece, 0, :, feeds], gain[piece, 1, :, feeds]

        def one(tile, total):
            lanes = pl.ds(pl.multiple_of(tile * 128, 128), 128)
            parts = [recv[piece, octet * 8 + s, :, lanes].astype(f32) for s in range(8)]
            parts = exchange(parts)
            for pol in range(POL):
                values = []
                for part in parts:
                    value = part[pol * 8 : pol * 8 + 8]
                    values.append(straight * value + crossed * pltpu.roll(value, QUARTER, 0))
                for n in range(0, 8, 2):
                    rows = pl.ds(pl.multiple_of(pol * 128 + tile * 64 + n * 8, LOCAL), LOCAL)
                    value = jnp.concatenate(values[n : n + 2], 0).astype(bf16)
                    cal[rows, feeds] = value
                    wide = value.astype(f32)
                    total = total + wide * wide
            return total

        return lax.fori_loop(0, 2, one, jnp.zeros((LOCAL, 128), f32))

    def arrive(piece, octet, count):
        pltpu.make_async_remote_copy(
            recv.at[piece, pl.ds(0, count)], recv.at[piece, pl.ds(0, count)],
            send_sem.at[piece], recv_sem.at[piece, octet],
            device_id={"shard": me}, device_id_type=MESH,
        ).wait_recv()

    def level_copy(piece, i):
        return pltpu.make_async_remote_copy(
            level_send.at[piece], level_recv.at[piece, place], level_send_sem.at[piece, i - 1],
            level_recv_sem.at[piece, place],
            device_id={"section": (place + i) % BLOCKS}, device_id_type=MESH,
        )

    def send_two_one(piece, dest):
        pltpu.make_async_remote_copy(
            send_two.at[piece, dest], recv_two.at[piece, me], send_two_sem.at[piece],
            recv_two_sem.at[piece], device_id={"shard": dest}, device_id_type=MESH,
        ).start()

    own_two = [
        pltpu.make_async_copy(
            send_two.at[piece, me], recv_two.at[piece, me], own_sem.at[PIECES + piece]
        )
        for piece in range(PIECES)
    ]
    factors = frame_matrix()
    evens = [1, 3, 5, 1 + MODF, 3 + MODF, 5 + MODF, None, None]
    odds = [0, 2, 4, 6, MODF, 2 + MODF, 4 + MODF, 6 + MODF]

    def pair(first, second):
        return jnp.where(lower, np.float32(first), np.float32(second))

    for piece in range(PIECES):

        def octets(i, total):
            octet = plane_of(i)
            arrive(piece, octet, 8)
            return total + calibrate(piece, octet)

        total = lax.fori_loop(0, 7, octets, jnp.zeros((LOCAL, 128), f32))
        arrive(piece, my_z, 7)
        own[piece].wait()
        total = total + calibrate(piece, my_z)
        total = total[:8] + total[8:]
        total = total + pltpu.roll(total, QUARTER, 0)
        total = jnp.sum(total, axis=1, keepdims=True) * (1.0 / TDFT) + 1e-06
        level_send[piece] = jnp.broadcast_to(total, (8, 128))
        level_recv[piece, place] = jnp.broadcast_to(total, (8, 128))

        decay_row = jnp.broadcast_to(decay_ref[...], (8, LOCAL))
        decay = jnp.sum(jnp.where(chan_pick(piece), decay_row, 0.0), axis=1, keepdims=True)
        decay = jnp.broadcast_to(decay, (8, 128))

        def beams(i, carry):
            wide = pl.ds(pl.multiple_of(i * 256, 256), 256)
            straight = dot(cal[...], beam_tab[0, :, wide]).reshape(32, 8, 256)
            crossed = dot(cal[...], beam_tab[1, :, wide]).reshape(32, 8, 256)
            value = straight + pltpu.roll(crossed, QUARTER, 1) * sign[:, :1]
            value = value * value
            value = value[:TDFT] + value[TDFT:]
            power[i] = value + pltpu.roll(value, QUARTER, 1)
            return carry

        for i in range(1, BLOCKS):
            level_copy(piece, i).start()
        lax.fori_loop(0, 4, beams, 0)
        for i in range(1, BLOCKS):
            other = (place + i) % BLOCKS
            pltpu.make_async_remote_copy(
                level_send.at[piece], level_recv.at[piece, other], level_send_sem.at[piece, i - 1],
                level_recv_sem.at[piece, other],
                device_id={"section": other}, device_id_type=MESH,
            ).wait_recv()
        dividend = jnp.zeros((8, 128), f32)
        divisor = jnp.zeros((8, 128), f32)
        for block in range(BLOCKS):
            use = block <= place
            dividend = jnp.where(use, decay * dividend + level_recv[piece, block], dividend)
            divisor = jnp.where(use, decay * divisor + 1.0, divisor)
        scale = divisor / dividend

        def modulate(i, carry):
            for tile in range(2):
                lanes = slice(tile * 128, (tile + 1) * 128)
                frames = []
                for n in range(TDFT // 2):
                    later = power[i, n + TDFT // 2, :, lanes]
                    frames.append(power[i, n, :, lanes] - sign * later)
                freqs = []
                for q_even, q_odd in zip(evens, odds):
                    column_even = np.zeros(TDFT) if q_even is None else factors[:, q_even]
                    column_odd = factors[:, q_odd]
                    value = None
                    for n in range(TDFT // 2):
                        first, second = float(column_even[n]), float(column_odd[n])
                        if max(abs(first), abs(second)) < 1e-12:
                            continue
                        term = frames[n] * pair(first, second)
                        value = term if value is None else value + term
                    freqs.append(value * scale - pair(column_even.sum(), column_odd.sum()))
                for j, part in enumerate(exchange(freqs)):
                    send_two[piece, i * 16 + tile * 8 + j] = part.astype(bf16)
            return carry

        lax.fori_loop(0, 4, modulate, 0)

        def two_plane(i, carry):
            z = plane_of(i)

            def one(r, inner):
                send_two_one(piece, z * 8 + (low + r) % 8)
                return inner

            return lax.fori_loop(0, 8, one, carry)

        lax.fori_loop(0, 7, two_plane, 0)

        def two_last(r, carry):
            send_two_one(piece, my_z * 8 + (low + r) % 8)
            return carry

        lax.fori_loop(1, 8, two_last, 0)
        own_two[piece].start()

    for piece in range(PIECES):
        pltpu.make_async_remote_copy(
            recv_two.at[piece, pl.ds(0, SHARDS - 1)], recv_two.at[piece, pl.ds(0, SHARDS - 1)],
            send_two_sem.at[piece], recv_two_sem.at[piece],
            device_id={"shard": me}, device_id_type=MESH,
        ).wait_recv()
        own_two[piece].wait()
        data = recv_two[piece].astype(f32).reshape(SHARDS // 2, 2, 8, 128)
        first, second = data[:, 0], data[:, 1]
        mask = lower[None]
        split = (
            jnp.where(mask, first, pltpu.roll(second, QUARTER, 1)),
            jnp.where(mask, pltpu.roll(first, QUARTER, 1), second),
        )
        for side in range(2):
            turned[side] = split[side].reshape(SHARDS * QUARTER, 128).T.astype(bf16)

        def dedisperse(g, carry):
            side, at = (g + 1) % 2, g // 2
            real = turned[side, pl.ds(pl.multiple_of(at * LOCAL, LOCAL), LOCAL), :]
            imag = turned[side, pl.ds(pl.multiple_of((at + 3 + side) * LOCAL, LOCAL), LOCAL), :]
            rows = slice(piece * 256, (piece + 1) * 256)
            total = dot(jnp.concatenate([real, imag], 0), phase[g, 0, rows, :])
            total = total + dot(jnp.concatenate([imag, -real], 0), phase[g, 1, rows, :])
            if piece > 0:
                total = total + total_ref[g]
            if piece < PIECES - 1:
                total_ref[g] = total
            else:
                out_ref[g] = (total * (1.0 / math.sqrt(CHANS))).astype(bf16)
            return carry

        lax.fori_loop(0, MODF, dedisperse, 0)

    for piece in range(PIECES):
        pltpu.make_async_remote_copy(
            send.at[piece, pl.ds(0, SHARDS - 1)], recv.at[piece, pl.ds(0, SHARDS - 1)],
            send_sem.at[piece], recv_sem.at[piece, 0],
            device_id={"shard": me}, device_id_type=MESH,
        ).wait_send()
        pltpu.make_async_remote_copy(
            send_two.at[piece, pl.ds(0, SHARDS - 1)], recv_two.at[piece, pl.ds(0, SHARDS - 1)],
            send_two_sem.at[piece], recv_two_sem.at[piece],
            device_id={"shard": me}, device_id_type=MESH,
        ).wait_send()
        for i in range(1, BLOCKS):
            level_copy(piece, i).wait_send()


def shards(voltages, feed_gains, grid_index, decay_rates, delays):
    bf16, f32 = jnp.bfloat16, jnp.float32
    anywhere = pl.BlockSpec(memory_space=pl.ANY)
    here = pl.BlockSpec(memory_space=pltpu.VMEM)
    dma = pltpu.SemaphoreType.DMA
    out = pl.pallas_call(
        body,
        out_shape=jax.ShapeDtypeStruct((MODF, 2 * LOCAL, TRIALS), bf16),
        in_specs=[anywhere] * 5 + [here] * 3,
        out_specs=here,
        scratch_shapes=[
            pltpu.VMEM((POL, LOCAL, TDFT * NSAMP), bf16),
            pltpu.VMEM((2, PIECE, NSAMP // 4), bf16),
            pltpu.VMEM((2, PIECE, NSAMP // 2), bf16),
            pltpu.VMEM((2, LOCAL, FEEDS), bf16),
            pltpu.VMEM((4, CHANS, 128), jnp.int32),
            pltpu.VMEM((2, ROWS, NSAMP // 4), bf16),
            pltpu.VMEM((ROWS, NSAMP // 2), bf16),
            pltpu.VMEM((PIECES, SHARDS, LOCAL, ROWS // 2), bf16),
            pltpu.VMEM((PIECES, SHARDS, LOCAL, ROWS // 2), bf16),
            pltpu.VMEM((PIECES, 2, 8, FEEDS), f32),
            pltpu.VMEM((POL * TDFT * 8, FEEDS), bf16),
            pltpu.VMEM((2, FEEDS, FEEDS), bf16),
            pltpu.VMEM((MODF, 2, CHANS, TRIALS), bf16),
            pltpu.VMEM((4, TDFT, 8, 256), f32),
            pltpu.VMEM((PIECES, SHARDS, 8, 128), bf16),
            pltpu.VMEM((PIECES, SHARDS, 8, 128), bf16),
            pltpu.VMEM((2, 128, SHARDS * QUARTER), bf16),
            pltpu.VMEM((MODF, 2 * LOCAL, TRIALS), f32),
            pltpu.VMEM((PIECES, 8, 128), f32),
            pltpu.VMEM((PIECES, BLOCKS, 8, 128), f32),
            dma((11,)), dma((2 * PIECES,)), dma((PIECES,)), dma((PIECES, 8)), dma((PIECES,)),
            dma((PIECES,)), dma((PIECES, BLOCKS - 1)), dma((PIECES, BLOCKS)),
        ],
        compiler_params=pltpu.CompilerParams(
            collective_id=0, has_side_effects=True, vmem_limit_bytes=VMEM_LIMIT
        ),
        name="telescope",
    )(
        voltages[0], spectral_constant(CLASSES[:2], NSAMP // 4),
        spectral_constant(CLASSES[2:], NSAMP // 2), feed_gains, delays,
        grid_index.reshape(8, 128), decay_rates.reshape(1, LOCAL), row_constant(),
    )
    return out.reshape(MODF, 2, LOCAL, TRIALS).transpose(0, 3, 1, 2)[None]


def solution(mesh):
    in_specs = (P("section", None, "shard", None), P(None, "shard", None), P(), P("shard"), P())
    out_specs = P("section", None, None, None, "shard")
    return jax.shard_map(shards, mesh=mesh, in_specs=in_specs, out_specs=out_specs, check_vma=False)
```

time: 83.4 us -> 79.6 us (0.954)
  Pallas kernels: 81.6 us -> 77.9 us
    pallas_call x1, Pallas kernels: 81.6 us -> 77.9 us  [shards(): pl.pallas_call(body, out_shape=jax.ShapeDtypeStruct((MODF, 2 * LOCAL, TRI...]
where the time goes in v3:
time: 79.6 us; the launch traced here: 79.5 us
  Pallas kernels  77.9 us (98%)
  local copies, waits for them, and re-layouts  1.64 us (2%)
    pallas_call x1, Pallas kernels, shards(): pl.pallas_call(body, out_shape=jax.ShapeDtypeStruct((MODF, 2 * LOCAL, TRI...  77.9 us
    unnamed x1, local copies, waits for them, and re-layouts  1.64 us

profile of v3, /device:TPU:1, one launch (start us, length us, event | category | flops | bytes accessed | tf_op | source)
XLA Modules:
  0.0 79.5 jit_solution(13183033267720046732)
XLA Ops:
  0.0 77.9 %telescope.1 = bf16[7,32,512]{2,1,0:T(8,128)(2,1)} custom-call(bf16[2,16,32768]{2,1,0:T(8,128)(2,1)} %bitcast.8, bf16[2,512,512]{2,1,0:T(8,128)(2,1)} %constant.12.even_hbm, bf16[2,512,1024]{2,1,0:T(8,128)(2,1)} %constant.13.odd_hbm, bf16[2,16,1024]{2,1,0:T(8,128)(2,1)} %gain_hbm.1, s32[1024,512]{1,0:T(8,128)} %delay_hbm.1, s32[8,128]{1,0:T(8,128)} %bitcast.10, ...), custom_call_target="tpu_custom_call" | custom-call | tf_op jit(solution)/shard_map/telescope/pallas_call | solution.py:489
  77.9 1.6 %copy.10 = bf16[1,7,512,2,16]{2,4,3,1,0:T(8,128)(2,1)} copy(bf16[1,7,512,2,16]{2,4,3,1,0:T(8,128)(2,1)} %bitcast.9) | data formatting | bytes 458752

commit v4 on v3

--- a/solution.py
+++ b/solution.py
@@ -87,8 +87,8 @@
 
 
 def body(
-    volts_hbm, even_hbm, odd_hbm, gain_hbm, delay_hbm, cell_ref, decay_ref, row_ref, out_ref,
-    volts, even, odd, gain_in, delay, fold_even, fold_odd, send, recv, gain, cal, beam_tab, phase, power,
+    volts_hbm, even_hbm, odd_hbm, gain_hbm, delay_hbm, cell_hbm, decay_hbm, row_hbm, out_ref,
+    volts, even, odd, gain_in, delay, cell_ref, decay_ref, row_ref, fold_even, fold_odd, send, recv, gain, cal, beam_tab, phase, power,
     send_two, recv_two, turned, total_ref, level_send, level_recv,
     load_sem, own_sem, send_sem, recv_sem, send_two_sem, recv_two_sem, level_send_sem, level_recv_sem,
 ):
@@ -113,7 +113,12 @@
         )
         for tile in range(4)
     ]
-    for load in load_volts + load_even + load_odd + [load_gain] + load_delay:
+    load_small = [
+        pltpu.make_async_copy(cell_hbm, cell_ref, load_sem.at[11]),
+        pltpu.make_async_copy(decay_hbm, decay_ref, load_sem.at[12]),
+        pltpu.make_async_copy(row_hbm, row_ref, load_sem.at[13]),
+    ]
+    for load in load_volts + load_even[:1]:
         load.start()
 
     barrier = pltpu.get_barrier_semaphore()
@@ -212,6 +217,8 @@
         load_volts[pol].wait()
         fold_sum(pol)
     load_even[0].wait()
+    for load in load_even[1:] + load_odd + [load_gain] + load_small + load_delay:
+        load.start()
     channelize(0)
     pl.semaphore_wait(barrier, SHARDS - 1 + BLOCKS - 1)
     send_piece(0)
@@ -234,6 +241,8 @@
     sign = jnp.where(lower, -1.0, 1.0).astype(f32)
 
     load_gain.wait()
+    for load in load_small:
+        load.wait()
     for piece in range(PIECES):
         pick = chan_pick(piece).astype(f32).astype(bf16)
         gain[piece, 0] = dot(pick, gain_in[0])
@@ -412,7 +421,7 @@
                     send_two[piece, i * 16 + tile * 8 + j] = part.astype(bf16)
             return carry
 
-        lax.fori_loop(0, 4, modulate, 0)
+        lax.fori_loop(0, 4, modulate, 0, unroll=piece == PIECES - 1)
 
         def two_plane(i, carry):
             z = plane_of(i)
@@ -421,7 +430,7 @@
                 send_two_one(piece, z * 8 + (low + r) % 8)
                 return inner
 
-            return lax.fori_loop(0, 8, one, carry)
+            return lax.fori_loop(0, 8, one, carry, unroll=piece == PIECES - 1)
 
         lax.fori_loop(0, 7, two_plane, 0)
 
@@ -464,7 +473,7 @@
                 out_ref[g] = (total * (1.0 / math.sqrt(CHANS))).astype(bf16)
             return carry
 
-        lax.fori_loop(0, MODF, dedisperse, 0)
+        lax.fori_loop(0, MODF, dedisperse, 0, unroll=piece == PIECES - 1)
 
     for piece in range(PIECES):
         pltpu.make_async_remote_copy(
@@ -483,13 +492,13 @@
 
 def shards(voltages, feed_gains, grid_index, decay_rates, delays):
     bf16, f32 = jnp.bfloat16, jnp.float32
-    anywhere = pl.BlockSpec(memory_space=pl.ANY)
+    far = pl.BlockSpec(memory_space=pltpu.HBM)
     here = pl.BlockSpec(memory_space=pltpu.VMEM)
     dma = pltpu.SemaphoreType.DMA
     out = pl.pallas_call(
         body,
         out_shape=jax.ShapeDtypeStruct((MODF, 2 * LOCAL, TRIALS), bf16),
-        in_specs=[anywhere] * 5 + [here] * 3,
+        in_specs=[far] * 8,
         out_specs=here,
         scratch_shapes=[
             pltpu.VMEM((POL, LOCAL, TDFT * NSAMP), bf16),
@@ -497,6 +506,9 @@
             pltpu.VMEM((2, PIECE, NSAMP // 2), bf16),
             pltpu.VMEM((2, LOCAL, FEEDS), bf16),
             pltpu.VMEM((4, CHANS, 128), jnp.int32),
+            pltpu.VMEM((8, 128), jnp.int32),
+            pltpu.VMEM((1, LOCAL), f32),
+            pltpu.VMEM((GRID_Y, 2 * GRID_Y), bf16),
             pltpu.VMEM((2, ROWS, NSAMP // 4), bf16),
             pltpu.VMEM((ROWS, NSAMP // 2), bf16),
             pltpu.VMEM((PIECES, SHARDS, LOCAL, ROWS // 2), bf16),
@@ -512,7 +524,7 @@
             pltpu.VMEM((MODF, 2 * LOCAL, TRIALS), f32),
             pltpu.VMEM((PIECES, 8, 128), f32),
             pltpu.VMEM((PIECES, BLOCKS, 8, 128), f32),
-            dma((11,)), dma((2 * PIECES,)), dma((PIECES,)), dma((PIECES, 8)), dma((PIECES,)),
+            dma((14,)), dma((2 * PIECES,)), dma((PIECES,)), dma((PIECES, 8)), dma((PIECES,)),
             dma((PIECES,)), dma((PIECES, BLOCKS - 1)), dma((PIECES, BLOCKS)),
         ],
         compiler_params=pltpu.CompilerParams(

time: 79.6 us -> 77.4 us (0.972)
  Pallas kernels: 77.9 us -> 75.6 us
    pallas_call x1, Pallas kernels: 77.9 us -> 75.6 us  [shards(): pl.pallas_call(body, out_shape=jax.ShapeDtypeStruct((MODF, 2 * LOCAL, TRI...]
where the time goes in v4:
time: 77.4 us; the launch traced here: 77.2 us
  Pallas kernels  75.6 us (98%)
  local copies, waits for them, and re-layouts  1.64 us (2%)
    pallas_call x1, Pallas kernels, shards(): pl.pallas_call(body, out_shape=jax.ShapeDtypeStruct((MODF, 2 * LOCAL, TRI...  75.6 us
    unnamed x1, local copies, waits for them, and re-layouts  1.64 us

profile of v4, /device:TPU:1, one launch (start us, length us, event | category | flops | bytes accessed | tf_op | source)
XLA Modules:
  0.0 77.2 jit_solution(5350200650872100810)
XLA Ops:
  0.0 75.6 %telescope.1 = bf16[7,32,512]{2,1,0:T(8,128)(2,1)} custom-call(bf16[2,16,32768]{2,1,0:T(8,128)(2,1)} %bitcast.8, bf16[2,512,512]{2,1,0:T(8,128)(2,1)} %constant.12.even_hbm, bf16[2,512,1024]{2,1,0:T(8,128)(2,1)} %constant.13.odd_hbm, bf16[2,16,1024]{2,1,0:T(8,128)(2,1)} %gain_hbm.1, s32[1024,512]{1,0:T(8,128)} %delay_hbm.1, s32[8,128]{1,0:T(8,128)} %bitcast.10, ...), custom_call_target="tpu_custom_call" | custom-call | tf_op jit(solution)/shard_map/telescope/pallas_call | solution.py:498
  75.6 1.6 %copy.10 = bf16[1,7,512,2,16]{2,4,3,1,0:T(8,128)(2,1)} copy(bf16[1,7,512,2,16]{2,4,3,1,0:T(8,128)(2,1)} %bitcast.9) | data formatting | bytes 458752

commit v5 on v4

--- a/solution.py
+++ b/solution.py
@@ -314,7 +314,7 @@
                     total = total + wide * wide
             return total
 
-        return lax.fori_loop(0, 2, one, jnp.zeros((LOCAL, 128), f32))
+        return lax.fori_loop(0, 2, one, jnp.zeros((LOCAL, 128), f32), unroll=True)
 
     def arrive(piece, octet, count):
         pltpu.make_async_remote_copy(

time: 77.4 us -> 77 us (level)
  no operation moved by 1% of the time
where the time goes in v5:
time: 77 us; the launch traced here: 76.9 us
  Pallas kernels  75.2 us (98%)
  local copies, waits for them, and re-layouts  1.64 us (2%)
    pallas_call x1, Pallas kernels, shards(): pl.pallas_call(body, out_shape=jax.ShapeDtypeStruct((MODF, 2 * LOCAL, TRI...  75.2 us
    unnamed x1, local copies, waits for them, and re-layouts  1.64 us

profile of v5, /device:TPU:1, one launch (start us, length us, event | category | flops | bytes accessed | tf_op | source)
XLA Modules:
  0.0 76.9 jit_solution(3214699789189743254)
XLA Ops:
  0.0 75.2 %telescope.1 = bf16[7,32,512]{2,1,0:T(8,128)(2,1)} custom-call(bf16[2,16,32768]{2,1,0:T(8,128)(2,1)} %bitcast.8, bf16[2,512,512]{2,1,0:T(8,128)(2,1)} %constant.12.even_hbm, bf16[2,512,1024]{2,1,0:T(8,128)(2,1)} %constant.13.odd_hbm, bf16[2,16,1024]{2,1,0:T(8,128)(2,1)} %gain_hbm.1, s32[1024,512]{1,0:T(8,128)} %delay_hbm.1, s32[8,128]{1,0:T(8,128)} %bitcast.10, ...), custom_call_target="tpu_custom_call" | custom-call | tf_op jit(solution)/shard_map/telescope/pallas_call | solution.py:498
  75.2 1.6 %copy.10 = bf16[1,7,512,2,16]{2,4,3,1,0:T(8,128)(2,1)} copy(bf16[1,7,512,2,16]{2,4,3,1,0:T(8,128)(2,1)} %bitcast.9) | data formatting | bytes 458752

commit v6 on v5

--- a/solution.py
+++ b/solution.py
@@ -109,12 +109,13 @@
     load_gain = pltpu.make_async_copy(gain_hbm, gain_in, load_sem.at[6])
     load_delay = [
         pltpu.make_async_copy(
-            delay_hbm.at[:, pl.ds(tile * 128, 128)], delay.at[tile], load_sem.at[7 + tile]
+            delay_hbm.at[:, pl.ds(tile * 128, 128)], delay.at[tile, pl.ds(0, CHANS)],
+            load_sem.at[7 + tile],
         )
         for tile in range(4)
     ]
     load_small = [
-        pltpu.make_async_copy(cell_hbm, cell_ref, load_sem.at[11]),
+        pltpu.make_async_copy(cell_hbm, cell_ref.at[pl.ds(0, 8)], load_sem.at[11]),
         pltpu.make_async_copy(decay_hbm, decay_ref, load_sem.at[12]),
         pltpu.make_async_copy(row_hbm, row_ref, load_sem.at[13]),
     ]
@@ -473,7 +474,7 @@
                 out_ref[g] = (total * (1.0 / math.sqrt(CHANS))).astype(bf16)
             return carry
 
-        lax.fori_loop(0, MODF, dedisperse, 0, unroll=piece == PIECES - 1)
+        lax.fori_loop(0, MODF, dedisperse, 0, unroll=piece >= PIECES - 2)
 
     for piece in range(PIECES):
         pltpu.make_async_remote_copy(
@@ -505,8 +506,8 @@
             pltpu.VMEM((2, PIECE, NSAMP // 4), bf16),
             pltpu.VMEM((2, PIECE, NSAMP // 2), bf16),
             pltpu.VMEM((2, LOCAL, FEEDS), bf16),
-            pltpu.VMEM((4, CHANS, 128), jnp.int32),
-            pltpu.VMEM((8, 128), jnp.int32),
+            pltpu.VMEM((4, CHANS + 8, 128), jnp.int32),
+            pltpu.VMEM((16, 128), jnp.int32),
             pltpu.VMEM((1, LOCAL), f32),
             pltpu.VMEM((GRID_Y, 2 * GRID_Y), bf16),
             pltpu.VMEM((2, ROWS, NSAMP // 4), bf16),

time: 77 us -> 77 us (level)
  no operation moved by 1% of the time
where the time goes in v6:
time: 77 us; the launch traced here: 76.9 us
  Pallas kernels  75.2 us (98%)
  local copies, waits for them, and re-layouts  1.64 us (2%)
    pallas_call x1, Pallas kernels, shards(): pl.pallas_call(body, out_shape=jax.ShapeDtypeStruct((MODF, 2 * LOCAL, TRI...  75.2 us
    unnamed x1, local copies, waits for them, and re-layouts  1.64 us

profile of v6, /device:TPU:1, one launch (start us, length us, event | category | flops | bytes accessed | tf_op | source)
XLA Modules:
  0.0 76.9 jit_solution(3793513096494212678)
XLA Ops:
  0.0 75.2 %telescope.1 = bf16[7,32,512]{2,1,0:T(8,128)(2,1)} custom-call(bf16[2,16,32768]{2,1,0:T(8,128)(2,1)} %bitcast.8, bf16[2,512,512]{2,1,0:T(8,128)(2,1)} %constant.12.even_hbm, bf16[2,512,1024]{2,1,0:T(8,128)(2,1)} %constant.13.odd_hbm, bf16[2,16,1024]{2,1,0:T(8,128)(2,1)} %gain_hbm.1, s32[1024,512]{1,0:T(8,128)} %delay_hbm.1, s32[8,128]{1,0:T(8,128)} %bitcast.10, ...), custom_call_target="tpu_custom_call" | custom-call | tf_op jit(solution)/shard_map/telescope/pallas_call | solution.py:499
  75.2 1.6 %copy.10 = bf16[1,7,512,2,16]{2,4,3,1,0:T(8,128)(2,1)} copy(bf16[1,7,512,2,16]{2,4,3,1,0:T(8,128)(2,1)} %bitcast.9) | data formatting | bytes 458752
